TPU v7x, 32 devices: a whole 2x2x4 slice. The times are simulated.
32 devices in a mesh: dp: 2 (over x), expert: 16 (over z, y, core).
Axes of the slice: x: 2, y: 2, z: 4, core: 2. Of those that a mesh axis runs over, the one named last changes fastest.
Arguments:
- tokens: bfloat16 [4096, 1024], P(('dp', 'expert')), may hold values from -6 to 6
- cotangent: bfloat16 [4096, 1024], P(('dp', 'expert')), may hold values from -6 to 6
- expert_ids: int32 [4096, 6], P(('dp', 'expert')), may hold values from 0 to 15, all different within a row; in each aligned block of 128 rows (0 to 127, 128 to 255, ...) at most 60 rows name the same one
- gate_weights: float32 [4096, 6], P(('dp', 'expert')), may hold values from 0.05 to 0.3
- partner: int32 [16], replicated, may hold values from 0 to 15, as said below
- weights: bfloat16 [16, 1024, 3, 384], P('expert', 'dp'), may hold values from -0.3125 to 0.3125
- first_moment: bfloat16 [16, 1024, 3, 384], P('expert', 'dp'), may hold values from -6 to 6
- second_moment: bfloat16 [16, 1024, 3, 384], P('expert', 'dp'), may hold values from 0.099609375 to 4
Outputs:
- mixed: bfloat16 [4096, 1024], P(('dp', 'expert'))
- token_grad: bfloat16 [4096, 1024], P(('dp', 'expert'))
- new_weights: bfloat16 [16, 1024, 3, 384], P('expert', 'dp')
- new_first: bfloat16 [16, 1024, 3, 384], P('expert', 'dp')
- new_second: bfloat16 [16, 1024, 3, 384], P('expert', 'dp')
Inputs may be any that keep to these rules, and one draw needn't show every extreme that they name: `expert_ids`: each row names 6 different experts. Among the 128 tokens of one device (aligned blocks of rows), no expert is named by more than 60 tokens, and in every draw some block names some expert exactly 60 times. partner[partner[h]] = h and partner[h] != h for every h.
All inputs are finite; a program needn't handle non-finite values.
Results may differ from a plain program's by a relative error of at most 0.024.
Values may be sent and summed in bfloat16 or wider, within the bound.
A program may use at most 64 MiB of HBM per device.

v0:
```python
import jax
import jax.numpy as jnp
from jax import lax
from jax.sharding import PartitionSpec as P

beta_one = 0.9
beta_two = 0.95
learn_rate = 0.01
decay_rate = 0.1
eps_adam = 1e-08
step_count = 100


def send_rows(parts):
    return (lax.all_to_all(parts[0], "expert", split_axis=0, concat_axis=0, tiled=True),)


def send_back(parts):
    return (lax.all_to_all(parts[0], "expert", split_axis=0, concat_axis=0, tiled=True),)


def shards(
    tokens, cotangent, expert_ids, gate_weights, partner, weights, first_moment, second_moment
):
    experts_here = lax.axis_size("expert")
    tok_dev, model_width = tokens.shape
    top_count = expert_ids.shape[1]
    hidden_width = weights.shape[3]
    capacity = min(tok_dev, max(2, 5 * tok_dev * top_count // (4 * experts_here)))
    item_total = tok_dev * top_count
    slot_total = experts_here * capacity
    flat_ids = expert_ids.reshape(item_total)
    onehot = (flat_ids[:, None] == jnp.arange(experts_here, dtype=jnp.int32)[None, :]).astype(
        jnp.int32
    )
    before = jnp.cumsum(onehot, axis=0) - onehot
    slot_of = jnp.sum(before * onehot, axis=1)
    position = flat_ids * capacity + slot_of
    source = (
        jnp.full((slot_total,), item_total, jnp.int32)
        .at[position]
        .set(jnp.arange(item_total, dtype=jnp.int32))
    )
    token_of = source // top_count
    zero_row = jnp.zeros((1, model_width), jnp.bfloat16)
    x_send = jnp.concatenate([tokens, zero_row], axis=0)[token_of].reshape(
        experts_here, capacity, model_width
    )
    gate_flat = gate_weights.reshape(item_total)
    gate_pad = jnp.concatenate([gate_flat, jnp.zeros((1,), jnp.float32)])
    cot_rows = jnp.concatenate([cotangent, zero_row], axis=0)[token_of].astype(jnp.float32)
    dy_send = (
        (gate_pad[source][:, None] * cot_rows)
        .astype(jnp.bfloat16)
        .reshape(experts_here, capacity, model_width)
    )
    gathered = lax.all_gather(weights, "dp", axis=1, tiled=True)[0]
    gate_up = gathered[:, 0:2, :].reshape(model_width, 2 * hidden_width)
    down_proj = gathered[:, 2, :]
    block_shape = (experts_here, capacity, model_width)
    (x_recv,) = send_rows((x_send,))
    forward_x_rows = x_recv.reshape(slot_total, model_width)
    both_proj = jnp.dot(forward_x_rows, gate_up, preferred_element_type=jnp.float32)
    pre_act = both_proj[:, :hidden_width]
    lin_act = both_proj[:, hidden_width:]
    sigmoid_pre = jax.nn.sigmoid(pre_act)
    silu_pre = pre_act * sigmoid_pre
    forward_hidden = (silu_pre * lin_act).astype(jnp.bfloat16)
    out_rows = jnp.dot(forward_hidden, down_proj.T, preferred_element_type=jnp.float32).astype(
        jnp.bfloat16
    )
    x_rows, saved, hidden, out_rows = (
        forward_x_rows,
        (pre_act, lin_act, sigmoid_pre, silu_pre),
        forward_hidden,
        out_rows,
    )
    (out_back,) = send_back((out_rows.reshape(block_shape),))
    (dy_recv,) = send_rows((dy_send,))
    pre_act, lin_act, sigmoid_pre, silu_pre = saved
    backward_dy_rows = dy_recv.reshape(slot_total, model_width)
    hidden_grad = jnp.dot(backward_dy_rows, down_proj, preferred_element_type=jnp.float32)
    pre_grad = (hidden_grad * lin_act * sigmoid_pre * (1.0 + pre_act * (1.0 - sigmoid_pre))).astype(
        jnp.bfloat16
    )
    lin_grad = (hidden_grad * silu_pre).astype(jnp.bfloat16)
    backward_both_grad = jnp.concatenate([pre_grad, lin_grad], axis=1)
    item_grad = jnp.dot(backward_both_grad, gate_up.T, preferred_element_type=jnp.float32).astype(
        jnp.bfloat16
    )
    dy_rows, both_grad, item_grad = (backward_dy_rows, backward_both_grad, item_grad)
    (grad_back,) = send_back((item_grad.reshape(block_shape),))
    out_items = (
        out_back.reshape(slot_total, model_width)[position].astype(jnp.float32) * gate_flat[:, None]
    )
    mixed = jnp.sum(out_items.reshape(tok_dev, top_count, model_width), axis=1).astype(jnp.bfloat16)
    grad_items = grad_back.reshape(slot_total, model_width)[position].astype(jnp.float32)
    token_grad = jnp.sum(grad_items.reshape(tok_dev, top_count, model_width), axis=1).astype(
        jnp.bfloat16
    )
    count = lax.axis_size("dp") * weights.shape[1]
    proj_grad = jnp.dot(x_rows.T, both_grad, preferred_element_type=jnp.float32)
    down_grad = jnp.dot(dy_rows.T, hidden, preferred_element_type=jnp.float32)
    grad_sum = lax.psum_scatter(
        jnp.concatenate(
            [proj_grad.reshape(count, 2, hidden_width), down_grad.reshape(count, 1, hidden_width)],
            axis=1,
        ).astype(jnp.bfloat16),
        "dp",
        scatter_dimension=0,
        tiled=True,
    ).astype(jnp.float32)
    w_old = weights[0].astype(jnp.float32)
    m_old = first_moment[0].astype(jnp.float32)
    v_old = second_moment[0].astype(jnp.float32)
    m_new = beta_one * m_old + (1.0 - beta_one) * grad_sum
    v_new = beta_two * v_old + (1.0 - beta_two) * grad_sum * grad_sum
    m_hat = m_new / (1.0 - beta_one**step_count)
    v_hat = v_new / (1.0 - beta_two**step_count)
    w_new = w_old - learn_rate * (m_hat / (jnp.sqrt(v_hat) + eps_adam) + decay_rate * w_old)
    pieces = (
        w_new.astype(jnp.bfloat16).reshape(experts_here, -1),
        m_new.astype(jnp.bfloat16).reshape(experts_here, -1),
        v_new.astype(jnp.bfloat16).reshape(experts_here, -1),
    )
    spread = (
        lax.all_to_all(pieces[0], "expert", split_axis=0, concat_axis=0, tiled=True),
        lax.all_to_all(pieces[1], "expert", split_axis=0, concat_axis=0, tiled=True),
        lax.all_to_all(pieces[2], "expert", split_axis=0, concat_axis=0, tiled=True),
    )
    ordered = (spread[0][partner], spread[1][partner], spread[2][partner])
    homed = (
        lax.all_to_all(ordered[0], "expert", split_axis=0, concat_axis=0, tiled=True),
        lax.all_to_all(ordered[1], "expert", split_axis=0, concat_axis=0, tiled=True),
        lax.all_to_all(ordered[2], "expert", split_axis=0, concat_axis=0, tiled=True),
    )
    new_weights = homed[0].reshape(weights.shape)
    new_first = homed[1].reshape(weights.shape)
    new_second = homed[2].reshape(weights.shape)
    return (mixed, token_grad, new_weights, new_first, new_second)


def solution(mesh):
    in_specs = (
        P(("dp", "expert"), None),
        P(("dp", "expert"), None),
        P(("dp", "expert"), None),
        P(("dp", "expert"), None),
        P(),
        P("expert", "dp", None, None),
        P("expert", "dp", None, None),
        P("expert", "dp", None, None),
    )
    out_specs = (
        P(("dp", "expert"), None),
        P(("dp", "expert"), None),
        P("expert", "dp", None, None),
        P("expert", "dp", None, None),
        P("expert", "dp", None, None),
    )
    return jax.shard_map(shards, mesh=mesh, in_specs=in_specs, out_specs=out_specs, check_vma=False)
```

profile of v0, /device:TPU:0, one launch (start us, length us, event | category | flops | bytes accessed | tf_op | source)
XLA Modules:
  0.0 497.3 jit_solution(16455755780328204852)
XLA Ops:
  21.5 7.5 %all-to-all-start = ((bf16[16,60,1024]{2,1,0:T(8,128)(2,1)}), bf16[16,60,1024]{2,1,0:T(8,128)(2,1)S(1)}, u32[]{:S(2)}, u32[]{:S(2)}) async-start(bf16[16,60,1024]{2,1,0:T(8,128)(2,1)} %reshape.150), calls=%async_computation | async-start | bytes 4194304 | tf_op jit(solution)/shard_map/all_to_all | solution.py:15
  47.3 22.8 %all-to-all-done = bf16[16,60,1024]{2,1,0:T(8,128)(2,1)S(1)} async-done(((bf16[16,60,1024]{2,1,0:T(8,128)(2,1)}), bf16[16,60,1024]{2,1,0:T(8,128)(2,1)S(1)}, u32[]{:S(2)}, u32[]{:S(2)}) %all-to-all-start) | async-done | bytes 1966112 | tf_op jit(solution)/shard_map/all_to_all | solution.py:15
  70.1 11.3 %all-to-all-start.2 = ((bf16[16,60,1024]{2,1,0:T(8,128)(2,1)}), bf16[16,60,1024]{2,1,0:T(8,128)(2,1)}, u32[]{:S(2)}, u32[]{:S(2)}) async-start(bf16[16,60,1024]{2,1,0:T(8,128)(2,1)} %multiply_convert_fusion), calls=%async_computation.2 | async-start | bytes 4194304 | tf_op jit(solution)/shard_map/all_to_all | solution.py:15
  82.9 38.8 %all-gather.2.cloned.1.call-done = bf16[1,1024,3,384]{1,3,2,0:T(8,128)(2,1)} async-done(((bf16[1,512,3,384]{1,3,2,0:T(8,128)(2,1)}), bf16[1,1024,3,384]{1,3,2,0:T(8,128)(2,1)}) %all-gather.2.cloned.1.call-update) | async-done | bytes 2359312 | tf_op jit(solution)/shard_map/all_gather | solution.py:57
  166.9 27.8 %all-to-all-done.3 = bf16[16,60,1024]{2,1,0:T(8,128)(2,1)} async-done(((bf16[16,60,1024]{2,1,0:T(8,128)(2,1)}), bf16[16,60,1024]{2,1,0:T(8,128)(2,1)}, u32[]{:S(2)}, u32[]{:S(2)}) %all-to-all-start.3) | async-done | bytes 1966112 | tf_op jit(solution)/shard_map/all_to_all | solution.py:19
  194.7 11.3 %all-to-all-start.1 = ((bf16[16,60,1024]{2,1,0:T(8,128)(2,1)}), bf16[16,60,1024]{2,1,0:T(8,128)(2,1)}, u32[]{:S(2)}, u32[]{:S(2)}) async-start(bf16[16,60,1024]{2,1,0:T(8,128)(2,1)} %reshape.153), calls=%async_computation.1 | async-start | bytes 4194304 | tf_op jit(solution)/shard_map/all_to_all | solution.py:19
  218.7 7.8 %reduce.10 = bf16[16,36864]{1,0:T(8,128)(2,1)S(1)} reduce(bf16[16,1,36864]{2,1,0:T(2,128)(2,1)S(1)} %all_to_all.74, bf16[]{:T(256)} %broadcast.129), dimensions={1}, to_apply=%all_to_all.74.reduce_sub_computation | reduce | bytes 2359298 | tf_op jit(solution)/shard_map/all_to_all | solution.py:128
  228.2 18.9 %all-to-all-done.1 = bf16[16,60,1024]{2,1,0:T(8,128)(2,1)} async-done(((bf16[16,60,1024]{2,1,0:T(8,128)(2,1)}), bf16[16,60,1024]{2,1,0:T(8,128)(2,1)}, u32[]{:S(2)}, u32[]{:S(2)}) %all-to-all-start.1) | async-done | bytes 1966112 | tf_op jit(solution)/shard_map/all_to_all | solution.py:19
  247.1 11.2 %all-to-all-start.6 = ((bf16[16,2,18432]{2,1,0:T(2,128)(2,1)}), bf16[16,2,18432]{2,1,0:T(2,128)(2,1)S(1)}, u32[]{:S(2)}, u32[]{:S(2)}) async-start(bf16[16,2,18432]{2,1,0:T(2,128)(2,1)} %reshape.257), calls=%async_computation.7 | async-start | bytes 2359296 | tf_op jit(solution)/shard_map/all_to_all | solution.py:128
  265.0 8.8 %reduce.12 = bf16[16,36864]{1,0:T(8,128)(2,1)} reduce(bf16[16,1,36864]{2,1,0:T(2,128)(2,1)S(1)} %all_to_all.75, bf16[]{:T(256)} %broadcast.129), dimensions={1}, to_apply=%all_to_all.75.reduce_sub_computation | reduce | bytes 2359298 | tf_op jit(solution)/shard_map/all_to_all | solution.py:129
  276.7 6.8 %all-to-all-done.6 = bf16[16,2,18432]{2,1,0:T(2,128)(2,1)S(1)} async-done(((bf16[16,2,18432]{2,1,0:T(2,128)(2,1)}), bf16[16,2,18432]{2,1,0:T(2,128)(2,1)S(1)}, u32[]{:S(2)}, u32[]{:S(2)}) %all-to-all-start.6) | async-done | bytes 1179680 | tf_op jit(solution)/shard_map/all_to_all | solution.py:128
  284.5 7.7 %all-to-all-start.8 = ((bf16[16,2,18432]{2,1,0:T(2,128)(2,1)}), bf16[16,2,18432]{2,1,0:T(2,128)(2,1)S(1)}, u32[]{:S(2)}, u32[]{:S(2)}) async-start(bf16[16,2,18432]{2,1,0:T(2,128)(2,1)} %reshape.261), calls=%async_computation.9 | async-start | bytes 2359296 | tf_op jit(solution)/shard_map/all_to_all | solution.py:129
  298.9 8.8 %reduce.8 = bf16[16,36864]{1,0:T(8,128)(2,1)} reduce(bf16[16,1,36864]{2,1,0:T(2,128)(2,1)S(1)} %all_to_all.73, bf16[]{:T(256)} %broadcast.129), dimensions={1}, to_apply=%all_to_all.73.reduce_sub_computation | reduce | bytes 2359298 | tf_op jit(solution)/shard_map/all_to_all | solution.py:127
  310.5 6.8 %all-to-all-done.8 = bf16[16,2,18432]{2,1,0:T(2,128)(2,1)S(1)} async-done(((bf16[16,2,18432]{2,1,0:T(2,128)(2,1)}), bf16[16,2,18432]{2,1,0:T(2,128)(2,1)S(1)}, u32[]{:S(2)}, u32[]{:S(2)}) %all-to-all-start.8) | async-done | bytes 1179680 | tf_op jit(solution)/shard_map/all_to_all | solution.py:129
  317.3 7.8 %all-to-all-start.4 = ((bf16[16,2,18432]{2,1,0:T(2,128)(2,1)}), bf16[16,2,18432]{2,1,0:T(2,128)(2,1)}, u32[]{:S(2)}, u32[]{:S(2)}) async-start(bf16[16,2,18432]{2,1,0:T(2,128)(2,1)} %reshape.253), calls=%async_computation.5 | async-start | bytes 2359296 | tf_op jit(solution)/shard_map/all_to_all | solution.py:127
  332.2 18.0 %all-to-all-done.4 = bf16[16,2,18432]{2,1,0:T(2,128)(2,1)} async-done(((bf16[16,2,18432]{2,1,0:T(2,128)(2,1)}), bf16[16,2,18432]{2,1,0:T(2,128)(2,1)}, u32[]{:S(2)}, u32[]{:S(2)}) %all-to-all-start.4) | async-done | bytes 1179680 | tf_op jit(solution)/shard_map/all_to_all | solution.py:127
  350.3 7.5 %all-to-all-start.7 = ((bf16[16,2,18432]{2,1,0:T(2,128)(2,1)}), bf16[16,2,18432]{2,1,0:T(2,128)(2,1)}, u32[]{:S(2)}, u32[]{:S(2)}) async-start(bf16[16,2,18432]{2,1,0:T(2,128)(2,1)} %reshape.259), calls=%async_computation.8 | async-start | bytes 2359296 | tf_op jit(solution)/shard_map/all_to_all | solution.py:134
  364.9 18.1 %all-to-all-done.7 = bf16[16,2,18432]{2,1,0:T(2,128)(2,1)} async-done(((bf16[16,2,18432]{2,1,0:T(2,128)(2,1)}), bf16[16,2,18432]{2,1,0:T(2,128)(2,1)}, u32[]{:S(2)}, u32[]{:S(2)}) %all-to-all-start.7) | async-done | bytes 1179680 | tf_op jit(solution)/shard_map/all_to_all | solution.py:134
  383.0 7.5 %all-to-all-start.9 = ((bf16[16,2,18432]{2,1,0:T(2,128)(2,1)}), bf16[16,2,18432]{2,1,0:T(2,128)(2,1)}, u32[]{:S(2)}, u32[]{:S(2)}) async-start(bf16[16,2,18432]{2,1,0:T(2,128)(2,1)} %reshape.263), calls=%async_computation.10 | async-start | bytes 2359296 | tf_op jit(solution)/shard_map/all_to_all | solution.py:135
  400.9 14.8 %all-to-all-done.9 = bf16[16,2,18432]{2,1,0:T(2,128)(2,1)} async-done(((bf16[16,2,18432]{2,1,0:T(2,128)(2,1)}), bf16[16,2,18432]{2,1,0:T(2,128)(2,1)}, u32[]{:S(2)}, u32[]{:S(2)}) %all-to-all-start.9) | async-done | bytes 1179680 | tf_op jit(solution)/shard_map/all_to_all | solution.py:135
  415.7 8.0 %all-to-all-start.5 = ((bf16[16,2,18432]{2,1,0:T(2,128)(2,1)}), bf16[16,2,18432]{2,1,0:T(2,128)(2,1)}, u32[]{:S(2)}, u32[]{:S(2)}) async-start(bf16[16,2,18432]{2,1,0:T(2,128)(2,1)} %reshape.255), calls=%async_computation.6 | async-start | bytes 2359296 | tf_op jit(solution)/shard_map/all_to_all | solution.py:133
  450.8 7.2 %reduce.4 = bf16[16,36864]{1,0:T(8,128)(2,1)S(1)} reduce(bf16[16,1,36864]{2,1,0:T(2,128)(2,1)S(1)} %reshape.260, bf16[]{:T(256)} %constant.67), dimensions={1}, to_apply=%all_to_all.67.reduce_sub_computation | reduce | bytes 2359298 | tf_op jit(solution)/shard_map/all_to_all | solution.py:134
  465.4 7.2 %reduce.5 = bf16[16,36864]{1,0:T(8,128)(2,1)S(1)} reduce(bf16[16,1,36864]{2,1,0:T(2,128)(2,1)S(1)} %reshape.264, bf16[]{:T(256)} %constant.67), dimensions={1}, to_apply=%all_to_all.72.reduce_sub_computation | reduce | bytes 2359298 | tf_op jit(solution)/shard_map/all_to_all | solution.py:135
  480.1 7.2 %reduce.3 = bf16[16,36864]{1,0:T(8,128)(2,1)S(1)} reduce(bf16[16,1,36864]{2,1,0:T(2,128)(2,1)S(1)} %reshape.256, bf16[]{:T(256)} %constant.67), dimensions={1}, to_apply=%all_to_all.62.reduce_sub_computation | reduce | bytes 2359298 | tf_op jit(solution)/shard_map/all_to_all | solution.py:133
  (135 shorter events, 182.9 us)
Async XLA Ops:
  21.5 7.5 %copy-start.15 = (bf16[128,1024]{1,0:T(8,128)(2,1)S(1)}, bf16[128,1024]{1,0:T(8,128)(2,1)}, u32[]{:S(2)}) copy-start(bf16[128,1024]{1,0:T(8,128)(2,1)} %param.9) | copy-start | bytes 786436
  21.5 48.6 %all-to-all-start = ((bf16[16,60,1024]{2,1,0:T(8,128)(2,1)}), bf16[16,60,1024]{2,1,0:T(8,128)(2,1)S(1)}, u32[]{:S(2)}, u32[]{:S(2)}) async-start(bf16[16,60,1024]{2,1,0:T(8,128)(2,1)} %reshape.150), calls=%async_computation | async-start | bytes 4194304 | tf_op jit(solution)/shard_map/all_to_all | solution.py:15
  34.4 3.8 copy-start.16
  47.3 34.2 %copy-start.4 = (bf16[1,512,3,384]{3,1,2,0:T(8,128)(2,1)S(1)}, bf16[1,512,3,384]{3,1,2,0:T(8,128)(2,1)}, u32[]{:S(2)}) copy-start(bf16[1,512,3,384]{3,1,2,0:T(8,128)(2,1)} %param.13) | copy-start | bytes 3538948
  70.1 61.1 %all-to-all-start.2 = ((bf16[16,60,1024]{2,1,0:T(8,128)(2,1)}), bf16[16,60,1024]{2,1,0:T(8,128)(2,1)}, u32[]{:S(2)}, u32[]{:S(2)}) async-start(bf16[16,60,1024]{2,1,0:T(8,128)(2,1)} %multiply_convert_fusion), calls=%async_computation.2 | async-start | bytes 4194304 | tf_op jit(solution)/shard_map/all_to_all | solution.py:15
  81.4 40.3 %all-gather.2.cloned.1.call-start = ((), (), s32[]{:S(2)}) async-start(), calls=%async_computation.11 | async-start | bytes 3538944 | tf_op jit(solution)/shard_map/all_gather | solution.py:57
  134.8 6.4 %copy-start.9 = (bf16[1024,2,384]{0,2,1:T(8,128)(2,1)S(1)}, bf16[1024,2,384]{0,2,1:T(8,128)(2,1)}, u32[]{:S(2)}) copy-start(bf16[1024,2,384]{0,2,1:T(8,128)(2,1)} %slice.41) | copy-start | bytes 4718596
  147.8 46.8 %all-to-all-start.3 = ((bf16[16,60,1024]{2,1,0:T(8,128)(2,1)}), bf16[16,60,1024]{2,1,0:T(8,128)(2,1)}, u32[]{:S(2)}, u32[]{:S(2)}) async-start(bf16[16,60,1024]{2,1,0:T(8,128)(2,1)} %reshape.157), calls=%async_computation.3 | async-start | bytes 4194304 | tf_op jit(solution)/shard_map/all_to_all | solution.py:19
  153.5 52.5 %reduce-scatter.2.cloned.1.call-start = ((), (), s32[]{:S(2)}) async-start(), calls=%async_computation.12 | async-start | bytes 3538944 | tf_op jit(solution)/shard_map/reduce_scatter | solution.py:104
  166.9 39.1 %copy-start.10 = (bf16[1,512,3,384]{3,1,2,0:T(8,128)(2,1)S(1)}, bf16[1,512,3,384]{3,1,2,0:T(8,128)(2,1)}, u32[]{:S(2)}) copy-start(bf16[1,512,3,384]{3,1,2,0:T(8,128)(2,1)} %param.15) | copy-start | bytes 3538948
  194.7 52.4 %all-to-all-start.1 = ((bf16[16,60,1024]{2,1,0:T(8,128)(2,1)}), bf16[16,60,1024]{2,1,0:T(8,128)(2,1)}, u32[]{:S(2)}, u32[]{:S(2)}) async-start(bf16[16,60,1024]{2,1,0:T(8,128)(2,1)} %reshape.153), calls=%async_computation.1 | async-start | bytes 4194304 | tf_op jit(solution)/shard_map/all_to_all | solution.py:19
  228.2 30.1 %copy-start.6 = (bf16[512,3,384]{2,0,1:T(8,128)(2,1)S(1)}, bf16[512,3,384]{2,0,1:T(8,128)(2,1)}, u32[]{:S(2)}) copy-start(bf16[512,3,384]{2,0,1:T(8,128)(2,1)} %get-tuple-element.28) | copy-start | bytes 3538948
  247.1 36.4 %all-to-all-start.6 = ((bf16[16,2,18432]{2,1,0:T(2,128)(2,1)}), bf16[16,2,18432]{2,1,0:T(2,128)(2,1)S(1)}, u32[]{:S(2)}, u32[]{:S(2)}) async-start(bf16[16,2,18432]{2,1,0:T(2,128)(2,1)} %reshape.257), calls=%async_computation.7 | async-start | bytes 2359296 | tf_op jit(solution)/shard_map/all_to_all | solution.py:128
  276.7 15.5 %copy-start.5 = (bf16[512,3,384]{2,0,1:T(8,128)(2,1)S(1)}, bf16[512,3,384]{2,0,1:T(8,128)(2,1)}, u32[]{:S(2)}) copy-start(bf16[512,3,384]{2,0,1:T(8,128)(2,1)} %get-tuple-element.29) | copy-start | bytes 3538948
  284.5 32.8 %all-to-all-start.8 = ((bf16[16,2,18432]{2,1,0:T(2,128)(2,1)}), bf16[16,2,18432]{2,1,0:T(2,128)(2,1)S(1)}, u32[]{:S(2)}, u32[]{:S(2)}) async-start(bf16[16,2,18432]{2,1,0:T(2,128)(2,1)} %reshape.261), calls=%async_computation.9 | async-start | bytes 2359296 | tf_op jit(solution)/shard_map/all_to_all | solution.py:129
  310.5 14.6 %copy-start.17 = (s32[16]{0:T(128)S(1)}, s32[16]{0:T(128)}, u32[]{:S(2)}) copy-start(s32[16]{0:T(128)} %param.12) | copy-start | bytes 196
  310.5 14.7 %copy-start.3 = (bf16[16,2,18432]{2,1,0:T(2,128)(2,1)S(1)}, bf16[16,2,18432]{2,1,0:T(2,128)(2,1)}, u32[]{:S(2)}) copy-start(bf16[16,2,18432]{2,1,0:T(2,128)(2,1)} %copy-done.2) | copy-start | bytes 3538948
  317.3 7.8 %copy-start = (bf16[16,2,18432]{2,1,0:T(2,128)(2,1)}, bf16[16,2,18432]{2,1,0:T(2,128)(2,1)S(1)}, u32[]{:S(2)}) copy-start(bf16[16,2,18432]{2,1,0:T(2,128)(2,1)S(1)} %all-to-all-done.8) | copy-start | bytes 3538948
  317.3 33.0 %all-to-all-start.4 = ((bf16[16,2,18432]{2,1,0:T(2,128)(2,1)}), bf16[16,2,18432]{2,1,0:T(2,128)(2,1)}, u32[]{:S(2)}, u32[]{:S(2)}) async-start(bf16[16,2,18432]{2,1,0:T(2,128)(2,1)} %reshape.253), calls=%async_computation.5 | async-start | bytes 2359296 | tf_op jit(solution)/shard_map/all_to_all | solution.py:127
  332.2 25.5 %copy-start.1 = (bf16[16,2,18432]{2,1,0:T(2,128)(2,1)S(1)}, bf16[16,2,18432]{2,1,0:T(2,128)(2,1)}, u32[]{:S(2)}) copy-start(bf16[16,2,18432]{2,1,0:T(2,128)(2,1)} %copy-done) | copy-start | bytes 3538948
  350.3 32.7 %all-to-all-start.7 = ((bf16[16,2,18432]{2,1,0:T(2,128)(2,1)}), bf16[16,2,18432]{2,1,0:T(2,128)(2,1)}, u32[]{:S(2)}, u32[]{:S(2)}) async-start(bf16[16,2,18432]{2,1,0:T(2,128)(2,1)} %reshape.259), calls=%async_computation.8 | async-start | bytes 2359296 | tf_op jit(solution)/shard_map/all_to_all | solution.py:134
  383.0 32.7 %all-to-all-start.9 = ((bf16[16,2,18432]{2,1,0:T(2,128)(2,1)}), bf16[16,2,18432]{2,1,0:T(2,128)(2,1)}, u32[]{:S(2)}, u32[]{:S(2)}) async-start(bf16[16,2,18432]{2,1,0:T(2,128)(2,1)} %reshape.263), calls=%async_computation.10 | async-start | bytes 2359296 | tf_op jit(solution)/shard_map/all_to_all | solution.py:135
  415.7 59.8 %all-to-all-start.5 = ((bf16[16,2,18432]{2,1,0:T(2,128)(2,1)}), bf16[16,2,18432]{2,1,0:T(2,128)(2,1)}, u32[]{:S(2)}, u32[]{:S(2)}) async-start(bf16[16,2,18432]{2,1,0:T(2,128)(2,1)} %reshape.255), calls=%async_computation.6 | async-start | bytes 2359296 | tf_op jit(solution)/shard_map/all_to_all | solution.py:133
  439.8 2.1 copy-start.14
  (7 other events, 9.3 us)
Sparse Core Ops, SparseCore 0:
  84.4 37.3 all-gather.1
  162.9 35.0 reduce-scatter.1
where the time goes:
time: 507 us; the launch traced here: 497 us
  waiting for transfers between devices  173 us (34%)
  local copies, waits for them, and re-layouts  131 us (26%)
  starting transfers between devices  86 us (17%)
  other arithmetic  73.2 us (14%)
  matrix products  19.3 us (4%)
  between operations  14.9 us (3%)
    all_to_all x2, waiting for transfers between devices, send_back(): lax.all_to_all(parts[0], 'expert', split_axis=0, concat_axis=0, tiled=True)  46.7 us
    unnamed x59, local copies, waits for them, and re-layouts  46.5 us
    all_gather x1, waiting for transfers between devices, shards(): gathered = lax.all_gather(weights, 'dp', axis=1, tiled=True)[0]  38.8 us
    all_to_all x2, waiting for transfers between devices, send_rows(): lax.all_to_all(parts[0], 'expert', split_axis=0, concat_axis=0, tiled=True)  22.8 us
    all_to_all x2, starting transfers between devices, send_rows(): lax.all_to_all(parts[0], 'expert', split_axis=0, concat_axis=0, tiled=True)  18.8 us
    all_to_all x1, waiting for transfers between devices, shards(): lax.all_to_all(ordered[1], 'expert', split_axis=0, concat_axis=0, tiled=T...  18.1 us
    all_to_all x1, waiting for transfers between devices, shards(): lax.all_to_all(pieces[0], 'expert', split_axis=0, concat_axis=0, tiled=True)  18 us
    all_to_all x2, starting transfers between devices, send_back(): lax.all_to_all(parts[0], 'expert', split_axis=0, concat_axis=0, tiled=True)  16.9 us
  transfers between devices with their start and end apart: 12, of which 9 were waited for; matrix products, arithmetic and copies ran while one was open for 33% of the time, Pallas kernels for 0%

commit v1 on v0

--- a/solution.py
+++ b/solution.py
@@ -19,7 +19,7 @@
     return (lax.all_to_all(parts[0], "expert", split_axis=0, concat_axis=0, tiled=True),)
 
 
-def shards(
+def shards_by_slot(
     tokens, cotangent, expert_ids, gate_weights, partner, weights, first_moment, second_moment
 ):
     experts_here = lax.axis_size("expert")
@@ -140,6 +140,78 @@
     return (mixed, token_grad, new_weights, new_first, new_second)
 
 
+def adam(w_old, m_old, v_old, grad_sum):
+    m_new = beta_one * m_old + (1.0 - beta_one) * grad_sum
+    v_new = beta_two * v_old + (1.0 - beta_two) * grad_sum * grad_sum
+    m_hat = m_new / (1.0 - beta_one**step_count)
+    v_hat = v_new / (1.0 - beta_two**step_count)
+    w_new = w_old - learn_rate * (m_hat / (jnp.sqrt(v_hat) + eps_adam) + decay_rate * w_old)
+    return w_new, m_new, v_new
+
+
+def shards_dense(
+    tokens, cotangent, expert_ids, gate_weights, partner, weights, first_moment, second_moment
+):
+    experts_here = lax.axis_size("expert")
+    me = lax.axis_index("expert")
+    tok_dev, model_width = tokens.shape
+    own_rows, hidden_width = weights.shape[1], weights.shape[3]
+    width = 3 * hidden_width
+    f32, bf16 = jnp.float32, jnp.bfloat16
+    hits = expert_ids[:, :, None] == jnp.arange(experts_here, dtype=jnp.int32)[None, None, :]
+    gate_table = jnp.sum(jnp.where(hits, gate_weights[:, :, None], 0.0), axis=1).T
+    w_flat = weights[0].reshape(own_rows, width)
+    gathered = lax.all_gather(w_flat, "dp", axis=0, tiled=True)
+    x_rows = lax.all_gather(tokens, "expert", axis=0, tiled=True)
+    cot_rows = lax.all_gather(cotangent, "expert", axis=0, tiled=True)
+    gate_all = lax.all_gather(gate_table, "expert", axis=0)
+    gate = lax.dynamic_index_in_dim(gate_all, me, 1, keepdims=False)
+    gate = gate.reshape(experts_here * tok_dev, 1)
+    gate_up = gathered[:, : 2 * hidden_width]
+    down_proj = gathered[:, 2 * hidden_width :]
+    both_proj = jnp.dot(x_rows, gate_up, preferred_element_type=f32)
+    pre_act = both_proj[:, :hidden_width]
+    lin_act = both_proj[:, hidden_width:]
+    sigmoid_pre = jax.nn.sigmoid(pre_act)
+    silu_pre = pre_act * sigmoid_pre
+    hidden = (silu_pre * lin_act).astype(bf16)
+    out_rows = jnp.dot(hidden, down_proj.T, preferred_element_type=f32)
+    mixed = lax.psum_scatter(
+        (gate * out_rows).astype(bf16), "expert", scatter_dimension=0, tiled=True
+    )
+    dy_rows = (gate * cot_rows.astype(f32)).astype(bf16)
+    hidden_grad = jnp.dot(dy_rows, down_proj, preferred_element_type=f32)
+    pre_grad = hidden_grad * lin_act * sigmoid_pre * (1.0 + pre_act * (1.0 - sigmoid_pre))
+    lin_grad = hidden_grad * silu_pre
+    both_grad = jnp.concatenate([pre_grad.astype(bf16), lin_grad.astype(bf16)], axis=1)
+    proj_grad = jnp.dot(x_rows.T, both_grad, preferred_element_type=f32)
+    down_grad = jnp.dot(dy_rows.T, hidden, preferred_element_type=f32)
+    partial = jnp.concatenate([proj_grad.astype(bf16), down_grad.astype(bf16)], axis=1)
+    grad_sum = lax.psum_scatter(partial, "dp", scatter_dimension=0, tiled=True).astype(f32)
+    item_grad = jnp.dot(both_grad, gate_up.T, preferred_element_type=f32).astype(bf16)
+    token_grad = lax.psum_scatter(item_grad, "expert", scatter_dimension=0, tiled=True)
+    m_flat = first_moment[0].reshape(own_rows, width)
+    v_flat = second_moment[0].reshape(own_rows, width)
+    new_state = adam(w_flat.astype(f32), m_flat.astype(f32), v_flat.astype(f32), grad_sum)
+    share = own_rows // experts_here
+    outs = []
+    for part in new_state:
+        pieces = part.astype(bf16).reshape(experts_here, share, width)
+        spread = lax.all_to_all(pieces, "expert", split_axis=0, concat_axis=0, tiled=True)
+        homed = lax.all_to_all(
+            spread[partner], "expert", split_axis=0, concat_axis=0, tiled=True
+        )
+        outs.append(homed.reshape(weights.shape))
+    return (mixed, token_grad, *outs)
+
+
+def shards(*args):
+    replica_rows = lax.axis_size("expert") * args[0].shape[0]
+    if replica_rows <= 4096 and args[5].shape[1] % (16 * lax.axis_size("expert")) == 0:
+        return shards_dense(*args)
+    return shards_by_slot(*args)
+
+
 def solution(mesh):
     in_specs = (
         P(("dp", "expert"), None),

time: 507 us -> 466 us (0.919); the launches traced: 497 us -> 464 us
  waiting for transfers between devices: 173 us -> 304 us
  local copies, waits for them, and re-layouts: 131 us -> 28.5 us
  other arithmetic: 73.2 us -> 9.51 us
  starting transfers between devices: 86 us -> 49 us
  blocking collectives: 0 us -> 23.4 us
  matrix products: 19.3 us -> 35.4 us
    all_gather x1 -> x3, waiting for transfers between devices: 38.8 us -> 110 us  [the longest x1 52.8 us: shards_dense(): x_rows = lax.all_gather(tokens, 'expert', axis=0, tiled=True)]
    all_to_all x9 -> x0, other arithmetic: 51.5 us -> none  [the longest x1 8.81 us: shards(): lax.all_to_all(pieces[2], 'expert', split_axis=0, concat_axis=0, tiled=True)]
    unnamed x59 -> x28, local copies, waits for them, and re-layouts: 46.5 us -> 9.09 us
    all_to_all x10 -> x6, starting transfers between devices: 85.5 us -> 48.8 us  [the longest x3 25.4 us: shards_dense(): lax.all_to_all(spread[partner], 'expert', split_axis=0, concat_axis=0, ti...]
    all_to_all x10 -> x6, waiting for transfers between devices: 134 us -> 167 us  [the longest x3 84 us: shards_dense(): lax.all_to_all(pieces, 'expert', split_axis=0, concat_axis=0, tiled=True)]
    reduce_scatter x1 -> x3, waiting for transfers between devices: 0.02 us -> 25.8 us  [the longest x1 25.8 us: shards_dense(): lax.psum_scatter(partial, 'dp', scatter_dimension=0, tiled=True).astype(f32)]
    all_gather x0 -> x1, blocking collectives: none -> 23.4 us  [shards_dense(): gate_all = lax.all_gather(gate_table, 'expert', axis=0)]
    gather x9 -> x3, local copies, waits for them, and re-layouts: 26.7 us -> 5.06 us  [shards_dense(): spread[partner]]
  transfers between devices with their start and end apart: 12 -> 12, of which waited for: 9 -> 10; matrix products, arithmetic and copies ran while one was open for 33% -> 10% of each run, Pallas kernels for 0% -> 0%
where the time goes in v1:
time: 466 us; the launch traced here: 464 us
  waiting for transfers between devices  304 us (65%)
  starting transfers between devices  49 us (11%)
  matrix products  35.4 us (8%)
  local copies, waits for them, and re-layouts  28.5 us (6%)
  blocking collectives  23.4 us (5%)
  between operations  14.4 us (3%)
  other arithmetic  9.51 us (2%)
    all_to_all x3, waiting for transfers between devices, shards_dense(): lax.all_to_all(pieces, 'expert', split_axis=0, concat_axis=0, tiled=True)  84 us
    all_to_all x3, waiting for transfers between devices, shards_dense(): lax.all_to_all(spread[partner], 'expert', split_axis=0, concat_axis=0, ti...  82.9 us
    all_gather x1, waiting for transfers between devices, shards_dense(): x_rows = lax.all_gather(tokens, 'expert', axis=0, tiled=True)  52.8 us
    all_gather x1, waiting for transfers between devices, shards_dense(): cot_rows = lax.all_gather(cotangent, 'expert', axis=0, tiled=True)  42.5 us
    reduce_scatter x1, waiting for transfers between devices, shards_dense(): lax.psum_scatter(partial, 'dp', scatter_dimension=0, tiled=True).astype(f32)  25.8 us
    all_to_all x3, starting transfers between devices, shards_dense(): lax.all_to_all(spread[partner], 'expert', split_axis=0, concat_axis=0, ti...  25.4 us
    all_gather x1, blocking collectives, shards_dense(): gate_all = lax.all_gather(gate_table, 'expert', axis=0)  23.4 us
    all_to_all x3, starting transfers between devices, shards_dense(): lax.all_to_all(pieces, 'expert', split_axis=0, concat_axis=0, tiled=True)  23.4 us
  transfers between devices with their start and end apart: 12, of which 10 were waited for; matrix products, arithmetic and copies ran while one was open for 10% of the time, Pallas kernels for 0%

profile of v1, /device:TPU:0, one launch (start us, length us, event | category | flops | bytes accessed | tf_op | source)
XLA Modules:
  0.0 463.8 jit_solution(3843170583067933573)
XLA Ops:
  7.2 2.4 copy.29
  11.2 23.4 %all-gather = f32[256,128]{1,0:T(8,128)S(1)} all-gather(f32[16,128]{1,0:T(8,128)S(1)} %bitcast.29), channel_id=2, replica_groups=mesh['dp'=2,'expert'=16] {'expert'}, dimensions={0}, use_global_device_ids=true | all-gather | bytes 139264 | tf_op jit(solution)/shard_map/all_gather | solution.py:167
  34.7 14.3 %all-gather.7.cloned.1.call-done = bf16[1024,1152]{0,1:T(8,128)(2,1)} async-done(((bf16[512,1152]{0,1:T(8,128)(2,1)}), bf16[1024,1152]{0,1:T(8,128)(2,1)}) %all-gather.7.cloned.1.call-update) | async-done | bytes 2359312 | tf_op jit(solution)/shard_map/all_gather | solution.py:164
  48.9 52.8 %all-gather.5.cloned.1.call-done = bf16[2048,1024]{1,0:T(8,128)(2,1)} async-done(((bf16[128,1024]{1,0:T(8,128)(2,1)}), bf16[2048,1024]{1,0:T(8,128)(2,1)}) %all-gather.5.cloned.1.call-update) | async-done | bytes 4194320 | tf_op jit(solution)/shard_map/all_gather | solution.py:165
  101.7 8.7 %fusion.14 = f32[2048,768]{0,1:T(8,128)} fusion(bf16[2048,1024]{1,0:T(8,128)(2,1)} %all-gather.5.cloned.1.call-done, bf16[1024,1152]{0,1:T(8,128)(2,1)} %all-gather.7.cloned.1.call-done), kind=kOutput, calls=%fused_computation.32 | convolution fusion | flops 3221225472 | bytes 12058624 | tf_op jit(solution)/shard_map/dot_general | solution.py:172
  110.4 42.5 %all-gather.9.cloned.1.call-done = bf16[2048,1024]{1,0:T(8,128)(2,1)} async-done(((bf16[128,1024]{1,0:T(8,128)(2,1)}), bf16[2048,1024]{1,0:T(8,128)(2,1)}) %all-gather.9.cloned.1.call-update) | async-done | bytes 4194320 | tf_op jit(solution)/shard_map/all_gather | solution.py:166
  153.0 7.5 %multiply_convert_fusion.3 = (bf16[2048,384]{0,1:T(8,128)(2,1)S(1)}, bf16[2048,384]{0,1:T(8,128)(2,1)S(1)}, bf16[2048,384]{0,1:T(8,128)(2,1)S(1)}) fusion(f32[2048,768]{0,1:T(8,128)} %fusion.14, bf16[1024,1152]{0,1:T(8,128)(2,1)} %all-gather.7.cloned.1.call-done, bf16[2048,1024]{1,0:T(8,128)(2,1)} %all-gather.9.cloned.1.call-done, f32[2048]{0:T(1024)S(1)} %bitcast.30), kind=kOutput, calls=%fused_computation.9 | convolution fusion | flops 1628700672 | bytes 15998976 | tf_op jit(solution)/shard_map/dot_general | solution.py:183
  164.4 3.4 fusion.10
  177.0 25.8 %reduce-scatter.8.cloned.1.call-done = bf16[512,1152]{0,1:T(8,128)(2,1)} async-done(((bf16[1024,1152]{0,1:T(8,128)(2,1)}), bf16[512,1152]{0,1:T(8,128)(2,1)}) %reduce-scatter.8.cloned.1.call-update) | async-done | bytes 1179664 | tf_op jit(solution)/shard_map/reduce_scatter | solution.py:190
  202.8 5.8 %fusion.16 = (bf16[512,1152]{0,1:T(8,128)(2,1)S(1)}, bf16[512,1152]{0,1:T(8,128)(2,1)}, bf16[512,1152]{0,1:T(8,128)(2,1)S(1)}) fusion(bf16[512,1152]{0,1:T(8,128)(2,1)} %reduce-scatter.8.cloned.1.call-done, f32[1,512,3,384]{1,3,2,0:T(8,128)} %copy.31, f32[1,512,3,384]{1,3,2,0:T(8,128)} %copy.30, bf16[1,512,3,384]{1,3,2,0:T(8,128)(2,1)S(1)} %copy-done), kind=kLoop, calls=%fused_computation.34 | loop fusion | flops 10616832 | bytes 10616832 | tf_op jit(solution)/shard_map/convert_element_type | solution.py:199
  211.0 5.6 %all-to-all-start = ((bf16[16,32,1152]{2,1,0:T(8,128)(2,1)}), bf16[16,32,1152]{2,1,0:T(8,128)(2,1)S(1)}, u32[]{:S(2)}, u32[]{:S(2)}) async-start(bf16[16,32,1152]{2,1,0:T(8,128)(2,1)} %bitcast.7), calls=%async_computation.3 | async-start | bytes 2359296 | tf_op jit(solution)/shard_map/all_to_all | solution.py:200
  216.7 7.8 %convolution_convert_fusion = bf16[2048,1024]{1,0:T(8,128)(2,1)} fusion(bf16[2048,384]{0,1:T(8,128)(2,1)} %copy-done.11, bf16[2048,384]{0,1:T(8,128)(2,1)} %copy-done.10, bf16[1024,1152]{0,1:T(8,128)(2,1)} %all-gather.7.cloned.1.call-done), kind=kOutput, calls=%fused_computation.5 | convolution fusion | flops 3229614080 | bytes 8912896 | tf_op jit(solution)/shard_map/dot_general | solution.py:191
  225.9 15.9 %all-to-all-done = bf16[16,32,1152]{2,1,0:T(8,128)(2,1)S(1)} async-done(((bf16[16,32,1152]{2,1,0:T(8,128)(2,1)}), bf16[16,32,1152]{2,1,0:T(8,128)(2,1)S(1)}, u32[]{:S(2)}, u32[]{:S(2)}) %all-to-all-start) | async-done | bytes 1179680 | tf_op jit(solution)/shard_map/all_to_all | solution.py:200
  241.8 7.5 %all-to-all-start.2 = ((bf16[16,32,1152]{2,1,0:T(8,128)(2,1)}), bf16[16,32,1152]{2,1,0:T(8,128)(2,1)S(1)}, u32[]{:S(2)}, u32[]{:S(2)}) async-start(bf16[16,32,1152]{2,1,0:T(8,128)(2,1)} %bitcast.8), calls=%async_computation.5 | async-start | bytes 2359296 | tf_op jit(solution)/shard_map/all_to_all | solution.py:200
  250.7 37.7 %all-to-all-done.2 = bf16[16,32,1152]{2,1,0:T(8,128)(2,1)S(1)} async-done(((bf16[16,32,1152]{2,1,0:T(8,128)(2,1)}), bf16[16,32,1152]{2,1,0:T(8,128)(2,1)S(1)}, u32[]{:S(2)}, u32[]{:S(2)}) %all-to-all-start.2) | async-done | bytes 1179680 | tf_op jit(solution)/shard_map/all_to_all | solution.py:200
  288.4 10.3 %all-to-all-start.4 = ((bf16[16,32,1152]{2,1,0:T(8,128)(2,1)}), bf16[16,32,1152]{2,1,0:T(8,128)(2,1)S(1)}, u32[]{:S(2)}, u32[]{:S(2)}) async-start(bf16[16,32,1152]{2,1,0:T(8,128)(2,1)} %bitcast.27), calls=%async_computation.7 | async-start | bytes 2359296 | tf_op jit(solution)/shard_map/all_to_all | solution.py:200
  300.4 30.4 %all-to-all-done.4 = bf16[16,32,1152]{2,1,0:T(8,128)(2,1)S(1)} async-done(((bf16[16,32,1152]{2,1,0:T(8,128)(2,1)}), bf16[16,32,1152]{2,1,0:T(8,128)(2,1)S(1)}, u32[]{:S(2)}, u32[]{:S(2)}) %all-to-all-start.4) | async-done | bytes 1179680 | tf_op jit(solution)/shard_map/all_to_all | solution.py:200
  330.8 7.3 %all-to-all-start.1 = ((bf16[16,32,1152]{2,1,0:T(8,128)(2,1)}), bf16[16,32,1152]{2,1,0:T(8,128)(2,1)S(1)}, u32[]{:S(2)}, u32[]{:S(2)}) async-start(bf16[16,32,1152]{2,1,0:T(8,128)(2,1)} %gather_fusion), calls=%async_computation.4 | async-start | bytes 2359296 | tf_op jit(solution)/shard_map/all_to_all | solution.py:201
  338.2 6.0 %multiply_convert_fusion.1 = bf16[2048,1024]{1,0:T(8,128)(2,1)} fusion(bf16[2048,384]{0,1:T(8,128)(2,1)} %copy-done.9, f32[2048]{0:T(1024)S(1)} %bitcast.32, bf16[1024,1152]{0,1:T(8,128)(2,1)} %all-gather.7.cloned.1.call-done), kind=kOutput, calls=%fused_computation.4 | convolution fusion | flops 1614807040 | bytes 6561792 | tf_op jit(solution)/shard_map/dot_general | solution.py:178
  345.9 17.4 %all-to-all-done.1 = bf16[16,32,1152]{2,1,0:T(8,128)(2,1)S(1)} async-done(((bf16[16,32,1152]{2,1,0:T(8,128)(2,1)}), bf16[16,32,1152]{2,1,0:T(8,128)(2,1)S(1)}, u32[]{:S(2)}, u32[]{:S(2)}) %all-to-all-start.1) | async-done | bytes 1179680 | tf_op jit(solution)/shard_map/all_to_all | solution.py:201
  363.3 7.5 %all-to-all-start.3 = ((bf16[16,32,1152]{2,1,0:T(8,128)(2,1)}), bf16[16,32,1152]{2,1,0:T(8,128)(2,1)}, u32[]{:S(2)}, u32[]{:S(2)}) async-start(bf16[16,32,1152]{2,1,0:T(8,128)(2,1)} %gather_fusion.1), calls=%async_computation.6 | async-start | bytes 2359296 | tf_op jit(solution)/shard_map/all_to_all | solution.py:201
  372.5 37.4 %all-to-all-done.3 = bf16[16,32,1152]{2,1,0:T(8,128)(2,1)} async-done(((bf16[16,32,1152]{2,1,0:T(8,128)(2,1)}), bf16[16,32,1152]{2,1,0:T(8,128)(2,1)}, u32[]{:S(2)}, u32[]{:S(2)}) %all-to-all-start.3) | async-done | bytes 1179680 | tf_op jit(solution)/shard_map/all_to_all | solution.py:201
  409.9 10.5 %all-to-all-start.5 = ((bf16[16,32,1152]{2,1,0:T(8,128)(2,1)}), bf16[16,32,1152]{2,1,0:T(8,128)(2,1)}, u32[]{:S(2)}, u32[]{:S(2)}) async-start(bf16[16,32,1152]{2,1,0:T(8,128)(2,1)} %gather_fusion.2), calls=%async_computation.8 | async-start | bytes 2359296 | tf_op jit(solution)/shard_map/all_to_all | solution.py:201
  425.5 28.1 %all-to-all-done.5 = bf16[16,32,1152]{2,1,0:T(8,128)(2,1)} async-done(((bf16[16,32,1152]{2,1,0:T(8,128)(2,1)}), bf16[16,32,1152]{2,1,0:T(8,128)(2,1)}, u32[]{:S(2)}, u32[]{:S(2)}) %all-to-all-start.5) | async-done | bytes 1179680 | tf_op jit(solution)/shard_map/all_to_all | solution.py:201
  (60 shorter events, 33.4 us)
Async XLA Ops:
  7.2 4.0 copy-start.5
  7.2 4.0 copy-start.4
  7.2 41.8 %all-gather.7.cloned.1.call-start = ((), (), s32[]{:S(2)}) async-start(), calls=%async_computation.10 | async-start | bytes 3538944 | tf_op jit(solution)/shard_map/all_gather | solution.py:164
  9.6 92.1 %all-gather.5.cloned.1.call-start = ((), (), s32[]{:S(2)}) async-start(), calls=%async_computation.9 | async-start | bytes 4456448 | tf_op jit(solution)/shard_map/all_gather | solution.py:165
  10.4 142.6 %all-gather.9.cloned.1.call-start = ((), (), s32[]{:S(2)}) async-start(), calls=%async_computation.12 | async-start | bytes 4456448 | tf_op jit(solution)/shard_map/all_gather | solution.py:166
  11.1 191.7 %reduce-scatter.8.cloned.1.call-start = ((), (), s32[]{:S(2)}) async-start(), calls=%async_computation.14 | async-start | bytes 3538944 | tf_op jit(solution)/shard_map/reduce_scatter | solution.py:190
  153.0 7.5 %copy-start.7 = (bf16[2048,1024]{1,0:T(8,128)(2,1)S(1)}, bf16[2048,1024]{1,0:T(8,128)(2,1)}, u32[]{:S(2)}) copy-start(bf16[2048,1024]{1,0:T(8,128)(2,1)} %all-gather.9.cloned.1.call-done) | copy-start | bytes 12582916
  160.4 2.0 copy-start.9
  160.5 2.0 copy-start.10
  160.5 2.4 copy-start.11
  160.5 3.9 copy-start.6
  169.4 1.3 copy-start.3
  175.0 27.8 %copy-start = (bf16[1,512,3,384]{1,3,2,0:T(8,128)(2,1)S(1)}, bf16[1,512,3,384]{1,3,2,0:T(8,128)(2,1)}, u32[]{:S(2)}) copy-start(bf16[1,512,3,384]{1,3,2,0:T(8,128)(2,1)} %copy.29) | copy-start | bytes 3538948
  211.0 30.8 %all-to-all-start = ((bf16[16,32,1152]{2,1,0:T(8,128)(2,1)}), bf16[16,32,1152]{2,1,0:T(8,128)(2,1)S(1)}, u32[]{:S(2)}, u32[]{:S(2)}) async-start(bf16[16,32,1152]{2,1,0:T(8,128)(2,1)} %bitcast.7), calls=%async_computation.3 | async-start | bytes 2359296 | tf_op jit(solution)/shard_map/all_to_all | solution.py:200
  216.6 240.3 %reduce-scatter.6.cloned.1.call-start = ((), (), s32[]{:S(2)}) async-start(), calls=%async_computation.13 | async-start | bytes 4456448 | tf_op jit(solution)/shard_map/reduce_scatter | solution.py:192
  241.8 46.7 %all-to-all-start.2 = ((bf16[16,32,1152]{2,1,0:T(8,128)(2,1)}), bf16[16,32,1152]{2,1,0:T(8,128)(2,1)S(1)}, u32[]{:S(2)}, u32[]{:S(2)}) async-start(bf16[16,32,1152]{2,1,0:T(8,128)(2,1)} %bitcast.8), calls=%async_computation.5 | async-start | bytes 2359296 | tf_op jit(solution)/shard_map/all_to_all | solution.py:200
  249.3 49.4 %copy-start.8 = (s32[16]{0:T(128)S(1)}, s32[16]{0:T(128)}, u32[]{:S(2)}) copy-start(s32[16]{0:T(128)} %param.12) | copy-start | bytes 196
  288.4 42.4 %all-to-all-start.4 = ((bf16[16,32,1152]{2,1,0:T(8,128)(2,1)}), bf16[16,32,1152]{2,1,0:T(8,128)(2,1)S(1)}, u32[]{:S(2)}, u32[]{:S(2)}) async-start(bf16[16,32,1152]{2,1,0:T(8,128)(2,1)} %bitcast.27), calls=%async_computation.7 | async-start | bytes 2359296 | tf_op jit(solution)/shard_map/all_to_all | solution.py:200
  330.8 32.5 %all-to-all-start.1 = ((bf16[16,32,1152]{2,1,0:T(8,128)(2,1)}), bf16[16,32,1152]{2,1,0:T(8,128)(2,1)S(1)}, u32[]{:S(2)}, u32[]{:S(2)}) async-start(bf16[16,32,1152]{2,1,0:T(8,128)(2,1)} %gather_fusion), calls=%async_computation.4 | async-start | bytes 2359296 | tf_op jit(solution)/shard_map/all_to_all | solution.py:201
  338.1 118.8 %reduce-scatter.4.cloned.1.call-start = ((), (), s32[]{:S(2)}) async-start(), calls=%async_computation.11 | async-start | bytes 4456448 | tf_op jit(solution)/shard_map/reduce_scatter | solution.py:179
  363.3 9.2 %copy-start.1 = (bf16[16,32,1152]{2,1,0:T(8,128)(2,1)}, bf16[16,32,1152]{2,1,0:T(8,128)(2,1)S(1)}, u32[]{:S(2)}) copy-start(bf16[16,32,1152]{2,1,0:T(8,128)(2,1)S(1)} %all-to-all-done.1) | copy-start | bytes 3538948
  363.3 46.7 %all-to-all-start.3 = ((bf16[16,32,1152]{2,1,0:T(8,128)(2,1)}), bf16[16,32,1152]{2,1,0:T(8,128)(2,1)}, u32[]{:S(2)}, u32[]{:S(2)}) async-start(bf16[16,32,1152]{2,1,0:T(8,128)(2,1)} %gather_fusion.1), calls=%async_computation.6 | async-start | bytes 2359296 | tf_op jit(solution)/shard_map/all_to_all | solution.py:201
  409.9 10.6 %copy-start.2 = (bf16[16,32,1152]{2,1,0:T(8,128)(2,1)S(1)}, bf16[16,32,1152]{2,1,0:T(8,128)(2,1)}, u32[]{:S(2)}) copy-start(bf16[16,32,1152]{2,1,0:T(8,128)(2,1)} %copy-done.1) | copy-start | bytes 3538948
  409.9 43.6 %all-to-all-start.5 = ((bf16[16,32,1152]{2,1,0:T(8,128)(2,1)}), bf16[16,32,1152]{2,1,0:T(8,128)(2,1)}, u32[]{:S(2)}, u32[]{:S(2)}) async-start(bf16[16,32,1152]{2,1,0:T(8,128)(2,1)} %gather_fusion.2), calls=%async_computation.8 | async-start | bytes 2359296 | tf_op jit(solution)/shard_map/all_to_all | solution.py:201
Sparse Core Ops, SparseCore 0:
  10.1 38.7 all-gather.6
  51.1 50.5 all-gather.4
  103.9 49.0 all-gather.8
  169.6 33.1 reduce-scatter.7
  224.6 95.5 reduce-scatter.5
  344.3 98.8 reduce-scatter.3

commit v2 on v1

--- a/solution.py
+++ b/solution.py
@@ -1,6 +1,10 @@
+import functools
+
 import jax
 import jax.numpy as jnp
 from jax import lax
+from jax.experimental import pallas as pl
+from jax.experimental.pallas import tpu as pltpu
 from jax.sharding import PartitionSpec as P
 
 beta_one = 0.9
@@ -149,59 +153,170 @@
     return w_new, m_new, v_new
 
 
+def move_kernel(n, count, with_table, *refs):
+    partner_ref, refs = refs[0], refs[1:]
+    states, refs = refs[:count], refs[count:]
+    if with_table:
+        table_ref, refs = refs[0], refs[1:]
+    homes, refs = refs[:count], refs[count:]
+    if with_table:
+        table_out, refs = refs[0], refs[1:]
+    spread, refs = refs[:count], refs[count:]
+    ordered, send_one, recv_one, send_two, recv_two = refs[:5]
+    me = lax.axis_index("expert")
+    share = states[0].shape[1] // n
+
+    def rows(number):
+        return pl.ds(pl.multiple_of(number * share, share), share)
+
+    def to_peer(src, dst, send_sem, recv_sem, step):
+        return pltpu.make_async_remote_copy(
+            src_ref=src,
+            dst_ref=dst,
+            send_sem=send_sem,
+            recv_sem=recv_sem,
+            device_id={"expert": lax.rem(me + step, n)},
+            device_id_type=pl.DeviceIdType.MESH,
+        )
+
+    def table_copy(step):
+        peer = lax.rem(me + step, n)
+        return to_peer(
+            table_ref.at[peer], table_out.at[me], refs[5].at[step], refs[6].at[step], step
+        )
+
+    def first(i, step):
+        peer = lax.rem(me + step, n)
+        return to_peer(
+            states[i].at[:, rows(peer), :],
+            spread[i].at[me],
+            send_one.at[i, step],
+            recv_one.at[i, step],
+            step,
+        )
+
+    def second(i, step):
+        peer = lax.rem(me + step, n)
+        return to_peer(
+            ordered.at[i, peer],
+            homes[i].at[:, rows(me), :],
+            send_two.at[i, step],
+            recv_two.at[i, step],
+            step,
+        )
+
+    def each(fn):
+        def body(step, carry):
+            fn(step)
+            return carry
+
+        lax.fori_loop(1, n, body, 0)
+
+    barrier = pltpu.get_barrier_semaphore()
+    each(
+        lambda step: pl.semaphore_signal(
+            barrier,
+            inc=1,
+            device_id={"expert": lax.rem(me + step, n)},
+            device_id_type=pl.DeviceIdType.MESH,
+        )
+    )
+    pl.semaphore_wait(barrier, n - 1)
+    if with_table:
+        each(lambda step: table_copy(step).start())
+        table_out[me] = table_ref[me]
+    for i in range(count):
+        each(lambda step: first(i, step).start())
+    for i in range(count):
+        spread[i][me] = states[i][:, rows(me), :]
+        each(lambda step: first(i, step).wait_recv())
+
+        def pick(home, carry):
+            ordered[i, home] = spread[i][partner_ref[home]]
+            return carry
+
+        lax.fori_loop(0, n, pick, 0)
+        each(lambda step: second(i, step).start())
+        homes[i][:, rows(me), :] = ordered[i, me]
+    if with_table:
+        each(lambda step: table_copy(step).wait())
+    for i in range(count):
+        each(lambda step: first(i, step).wait_send())
+        each(lambda step: second(i, step).wait())
+
+
+def move_states(states, partner, table, number):
+    n = lax.axis_size("expert")
+    count = len(states)
+    planes, own_rows, width = states[0].shape
+    share = own_rows // n
+    vmem = pl.BlockSpec(memory_space=pltpu.VMEM)
+    extra = [] if table is None else [table]
+    sems = [pltpu.SemaphoreType.DMA((count, n))] * 4
+    sems += [pltpu.SemaphoreType.DMA((n,))] * (2 * len(extra))
+    moved = 2 * count * planes * own_rows * width * 2
+    return pl.pallas_call(
+        functools.partial(move_kernel, n, count, bool(extra)),
+        out_shape=[jax.ShapeDtypeStruct(a.shape, a.dtype) for a in [*states, *extra]],
+        in_specs=[pl.BlockSpec(memory_space=pltpu.SMEM)] + [vmem] * (count + len(extra)),
+        out_specs=[vmem] * (count + len(extra)),
+        scratch_shapes=[
+            *[pltpu.VMEM((n, planes, share, width), jnp.bfloat16)] * count,
+            pltpu.VMEM((count, n, planes, share, width), jnp.bfloat16),
+            *sems,
+        ],
+        compiler_params=pltpu.CompilerParams(
+            collective_id=number, has_side_effects=True, vmem_limit_bytes=32 * 2**20
+        ),
+        cost_estimate=pl.CostEstimate(
+            flops=0, bytes_accessed=30 * moved, transcendentals=0
+        ),
+    )(partner, *states, *extra)
+
+
 def shards_dense(
     tokens, cotangent, expert_ids, gate_weights, partner, weights, first_moment, second_moment
 ):
     experts_here = lax.axis_size("expert")
-    me = lax.axis_index("expert")
     tok_dev, model_width = tokens.shape
     own_rows, hidden_width = weights.shape[1], weights.shape[3]
-    width = 3 * hidden_width
     f32, bf16 = jnp.float32, jnp.bfloat16
     hits = expert_ids[:, :, None] == jnp.arange(experts_here, dtype=jnp.int32)[None, None, :]
     gate_table = jnp.sum(jnp.where(hits, gate_weights[:, :, None], 0.0), axis=1).T
-    w_flat = weights[0].reshape(own_rows, width)
-    gathered = lax.all_gather(w_flat, "dp", axis=0, tiled=True)
+    gate_table = jnp.broadcast_to(gate_table[:, None, :], (experts_here, 8, tok_dev))
+    old = [a[0].transpose(1, 0, 2) for a in (weights, first_moment, second_moment)]
+    gathered = lax.all_gather(old[0], "dp", axis=1, tiled=True)
     x_rows = lax.all_gather(tokens, "expert", axis=0, tiled=True)
     cot_rows = lax.all_gather(cotangent, "expert", axis=0, tiled=True)
-    gate_all = lax.all_gather(gate_table, "expert", axis=0)
-    gate = lax.dynamic_index_in_dim(gate_all, me, 1, keepdims=False)
-    gate = gate.reshape(experts_here * tok_dev, 1)
-    gate_up = gathered[:, : 2 * hidden_width]
-    down_proj = gathered[:, 2 * hidden_width :]
+    *old_here, gate_all = move_states(old, partner, gate_table, 0)
+    gate = gate_all[:, 0, :].reshape(experts_here * tok_dev, 1)
+    gate_up = jnp.concatenate([gathered[0], gathered[1]], axis=1)
+    down_proj = gathered[2]
     both_proj = jnp.dot(x_rows, gate_up, preferred_element_type=f32)
     pre_act = both_proj[:, :hidden_width]
     lin_act = both_proj[:, hidden_width:]
     sigmoid_pre = jax.nn.sigmoid(pre_act)
     silu_pre = pre_act * sigmoid_pre
     hidden = (silu_pre * lin_act).astype(bf16)
+    dy_rows = (gate * cot_rows.astype(f32)).astype(bf16)
+    hidden_grad = jnp.dot(dy_rows, down_proj, preferred_element_type=f32)
+    pre_grad = hidden_grad * lin_act * sigmoid_pre * (1.0 + pre_act * (1.0 - sigmoid_pre))
+    pre_grad = pre_grad.astype(bf16)
+    lin_grad = (hidden_grad * silu_pre).astype(bf16)
+    both_grad = jnp.concatenate([pre_grad, lin_grad], axis=1)
+    proj_grad = jnp.dot(x_rows.T, both_grad, preferred_element_type=f32).astype(bf16)
+    down_grad = jnp.dot(dy_rows.T, hidden, preferred_element_type=f32).astype(bf16)
+    partial = jnp.stack([proj_grad[:, :hidden_width], proj_grad[:, hidden_width:], down_grad])
+    grad_sum = lax.psum_scatter(partial, "dp", scatter_dimension=1, tiled=True)
     out_rows = jnp.dot(hidden, down_proj.T, preferred_element_type=f32)
     mixed = lax.psum_scatter(
         (gate * out_rows).astype(bf16), "expert", scatter_dimension=0, tiled=True
     )
-    dy_rows = (gate * cot_rows.astype(f32)).astype(bf16)
-    hidden_grad = jnp.dot(dy_rows, down_proj, preferred_element_type=f32)
-    pre_grad = hidden_grad * lin_act * sigmoid_pre * (1.0 + pre_act * (1.0 - sigmoid_pre))
-    lin_grad = hidden_grad * silu_pre
-    both_grad = jnp.concatenate([pre_grad.astype(bf16), lin_grad.astype(bf16)], axis=1)
-    proj_grad = jnp.dot(x_rows.T, both_grad, preferred_element_type=f32)
-    down_grad = jnp.dot(dy_rows.T, hidden, preferred_element_type=f32)
-    partial = jnp.concatenate([proj_grad.astype(bf16), down_grad.astype(bf16)], axis=1)
-    grad_sum = lax.psum_scatter(partial, "dp", scatter_dimension=0, tiled=True).astype(f32)
     item_grad = jnp.dot(both_grad, gate_up.T, preferred_element_type=f32).astype(bf16)
     token_grad = lax.psum_scatter(item_grad, "expert", scatter_dimension=0, tiled=True)
-    m_flat = first_moment[0].reshape(own_rows, width)
-    v_flat = second_moment[0].reshape(own_rows, width)
-    new_state = adam(w_flat.astype(f32), m_flat.astype(f32), v_flat.astype(f32), grad_sum)
-    share = own_rows // experts_here
-    outs = []
-    for part in new_state:
-        pieces = part.astype(bf16).reshape(experts_here, share, width)
-        spread = lax.all_to_all(pieces, "expert", split_axis=0, concat_axis=0, tiled=True)
-        homed = lax.all_to_all(
-            spread[partner], "expert", split_axis=0, concat_axis=0, tiled=True
-        )
-        outs.append(homed.reshape(weights.shape))
+    (grad_here,) = move_states([grad_sum], partner, None, 1)
+    new_state = adam(*[a.astype(f32) for a in old_here], grad_here.astype(f32))
+    outs = [a.astype(bf16).transpose(1, 0, 2)[None] for a in new_state]
     return (mixed, token_grad, *outs)
 
 

time: 466 us -> 468 us (level)
  Pallas kernels: 0 us -> 258 us
  waiting for transfers between devices: 304 us -> 144 us
  starting transfers between devices: 49 us -> 0.24 us
  blocking collectives: 23.4 us -> 0 us
  local copies, waits for them, and re-layouts: 28.5 us -> 8.25 us
    pallas_call x0 -> x2, Pallas kernels: none -> 258 us  [move_states(): pl.pallas_call(functools.partial(move_kernel, n, count, bool(extra)), out...]
    all_to_all x6 -> x0, waiting for transfers between devices: 167 us -> none  [the longest x3 84 us: shards_dense(): lax.all_to_all(pieces, 'expert', split_axis=0, concat_axis=0, tiled=True)]
    reduce_scatter x1, waiting for transfers between devices: 0.01 us -> 76.2 us  [shards_dense(): lax.psum_scatter((gate * out_rows).astype(bf16), 'expert', scatter_dimens...]
    all_gather x1, waiting for transfers between devices: 52.8 us -> 0.01 us  [shards_dense(): x_rows = lax.all_gather(tokens, 'expert', axis=0, tiled=True)]
    all_to_all x6 -> x0, starting transfers between devices: 48.8 us -> none  [the longest x3 25.4 us: shards_dense(): lax.all_to_all(spread[partner], 'expert', split_axis=0, concat_axis=0, ti...]
    all_gather x1, waiting for transfers between devices: 42.5 us -> 0.01 us  [shards_dense(): cot_rows = lax.all_gather(cotangent, 'expert', axis=0, tiled=True)]
    reduce_scatter x1, waiting for transfers between devices: 0.01 us -> 34.8 us  [shards_dense(): lax.psum_scatter(item_grad, 'expert', scatter_dimension=0, tiled=True)]
    all_gather x1 -> x0, blocking collectives: 23.4 us -> none  [shards_dense(): gate_all = lax.all_gather(gate_table, 'expert', axis=0)]
  transfers between devices with their start and end apart: 12 -> 6, of which waited for: 10 -> 3; matrix products, arithmetic and copies ran while one was open for 10% -> 6% of each run, Pallas kernels for 0% -> 55%
where the time goes in v2:
time: 468 us
  Pallas kernels  258 us (55%)
  waiting for transfers between devices  144 us (31%)
  matrix products  36.4 us (8%)
  between operations  14.3 us (3%)
  local copies, waits for them, and re-layouts  8.25 us (2%)
  other arithmetic  6.99 us (1%)
    pallas_call x2, Pallas kernels, move_states(): pl.pallas_call(functools.partial(move_kernel, n, count, bool(extra)), out...  258 us
    reduce_scatter x1, waiting for transfers between devices, shards_dense(): lax.psum_scatter((gate * out_rows).astype(bf16), 'expert', scatter_dimens...  76.2 us
    reduce_scatter x1, waiting for transfers between devices, shards_dense(): lax.psum_scatter(item_grad, 'expert', scatter_dimension=0, tiled=True)  34.8 us
    reduce_scatter x1, waiting for transfers between devices, shards_dense(): grad_sum = lax.psum_scatter(partial, 'dp', scatter_dimension=1, tiled=True)  31 us
  transfers between devices with their start and end apart: 6, of which 3 were waited for; matrix products, arithmetic and copies ran while one was open for 6% of the time, Pallas kernels for 55%

profile of v2, /device:TPU:0, one launch (start us, length us, event | category | flops | bytes accessed | tf_op | source)
XLA Modules:
  0.0 467.8 jit_solution(16469767402561410248)
XLA Ops:
  7.2 0.7 all-gather.4.cloned.1.call-update
  8.0 0.7 all-gather.6.cloned.1.call-update
  8.7 0.7 all-gather.8.cloned.1.call-update
  9.4 0.7 select_reduce_fusion
  10.2 1.3 copy-done.2
  11.5 1.3 copy-done.3
  12.7 0.7 copy-done.6
  13.4 203.5 %shard_map.119 = (bf16[3,512,384]{2,1,0:T(8,128)(2,1)S(1)}, bf16[3,512,384]{2,1,0:T(8,128)(2,1)S(1)}, bf16[3,512,384]{2,1,0:T(8,128)(2,1)S(1)}, f32[16,8,128]{2,1,0:T(8,128)S(1)}) custom-call(s32[16]{0:T(128)S(1)} %copy-done.6, bf16[3,512,384]{2,1,0:T(8,128)(2,1)S(1)} %bitcast.48, bf16[3,512,384]{2,1,0:T(8,128)(2,1)S(1)} %bitcast.49, ...), custom_call_target="tpu_custom_call" | custom-call | bytes 212336640 | tf_op jit(solution)/shard_map/pallas_call | solution.py:258
  216.9 1.0 copy-done.4
  217.9 2.4 slice_bitcast_fusion.4
  220.4 8.6 %convolution_bitcast_fusion = f32[2048,768]{0,1:T(8,128)} fusion(bf16[2048,1024]{1,0:T(8,128)(2,1)} %all-gather.6.cloned.1.call-done, bf16[1024,384]{1,0:T(8,128)(2,1)} %get-tuple-element.20, bf16[1024,384]{1,0:T(8,128)(2,1)S(1)} %get-tuple-element.19), kind=kOutput, calls=%fused_computation.2 | convolution fusion | flops 3224371200 | bytes 12058624 | tf_op jit(solution)/shard_map/dot_general | solution.py:295
  228.9 7.8 %multiply_convert_fusion.3 = (bf16[2048,384]{0,1:T(8,128)(2,1)S(1)}, bf16[2048,384]{0,1:T(8,128)(2,1)S(1)}, bf16[2048,384]{0,1:T(8,128)(2,1)S(1)}) fusion(f32[2048,768]{0,1:T(8,128)} %convolution_bitcast_fusion, bf16[3,1024,384]{2,1,0:T(8,128)(2,1)} %all-gather.4.cloned.1.call-done, bf16[2048,1024]{1,0:T(8,128)(2,1)} %all-gather.8.cloned.1.call-done, ...), kind=kOutput, calls=%fused_computation.7 | convolution fusion | flops 1628700672 | bytes 15998976 | tf_op jit(solution)/shard_map/dot_general | solution.py:302
  236.8 3.5 fusion.12
  240.5 0.2 copy-done.9
  240.6 3.0 fusion.14
  243.6 1.8 pad_maximum_fusion.1
  245.5 7.5 %convolution_convert_fusion = bf16[2048,1024]{1,0:T(8,128)(2,1)} fusion(bf16[2048,384]{0,1:T(8,128)(2,1)} %copy-done.12, bf16[2048,384]{0,1:T(8,128)(2,1)} %copy-done.11, bf16[1024,384]{1,0:T(8,128)(2,1)} %get-tuple-element.20, bf16[1024,384]{1,0:T(8,128)(2,1)S(1)} %get-tuple-element.19), kind=kOutput, calls=%fused_computation.3 | convolution fusion | flops 3232759808 | bytes 8912896 | tf_op jit(solution)/shard_map/dot_general | solution.py:315
  253.1 6.0 %multiply_convert_fusion.1 = bf16[2048,1024]{1,0:T(8,128)(2,1)} fusion(bf16[2048,384]{0,1:T(8,128)(2,1)} %copy-done.10, f32[2048]{0:T(1024)S(1)} %bitcast.54, bf16[3,1024,384]{2,1,0:T(8,128)(2,1)} %all-gather.4.cloned.1.call-done), kind=kOutput, calls=%fused_computation.1 | convolution fusion | flops 1614807040 | bytes 6561792 | tf_op jit(solution)/shard_map/dot_general | solution.py:311
  259.2 31.0 %reduce-scatter.8.cloned.1.call-done.refs_1_ = bf16[3,512,384]{2,1,0:T(8,128)(2,1)} async-done(((bf16[3,1024,384]{2,1,0:T(8,128)(2,1)}), bf16[3,512,384]{2,1,0:T(8,128)(2,1)}) %reduce-scatter.8.cloned.1.call-update) | async-done | bytes 1179664 | tf_op jit(solution)/shard_map/reduce_scatter | solution.py:310
  290.1 1.3 copy-done.1
  291.4 54.1 %shard_map.120 = bf16[3,512,384]{2,1,0:T(8,128)(2,1)S(1)} custom-call(s32[16]{0:T(128)S(1)} %copy-done.7, bf16[3,512,384]{2,1,0:T(8,128)(2,1)S(1)} %copy-done.1), custom_call_target="tpu_custom_call" | custom-call | bytes 70778880 | tf_op jit(solution)/shard_map/pallas_call | solution.py:258
  345.5 4.5 fusion.15
  350.0 34.8 %reduce-scatter.6.cloned.1.call-done = bf16[128,1024]{1,0:T(8,128)(2,1)} async-done(((bf16[2048,1024]{1,0:T(8,128)(2,1)}), bf16[128,1024]{1,0:T(8,128)(2,1)}) %reduce-scatter.6.cloned.1.call-update) | async-done | bytes 262160 | tf_op jit(solution)/shard_map/reduce_scatter | solution.py:316
  384.8 76.2 %reduce-scatter.4.cloned.1.call-done = bf16[128,1024]{1,0:T(8,128)(2,1)} async-done(((bf16[2048,1024]{1,0:T(8,128)(2,1)}), bf16[128,1024]{1,0:T(8,128)(2,1)}) %reduce-scatter.4.cloned.1.call-update) | async-done | bytes 262160 | tf_op jit(solution)/shard_map/reduce_scatter | solution.py:312
  (35 shorter events, 0.5 us)
Async XLA Ops:
  7.2 3.0 copy-start
  7.2 210.8 %all-gather.4.cloned.1.call-start = ((), (), s32[]{:S(2)}) async-start(), calls=%async_computation.3 | async-start | bytes 3538944 | tf_op jit(solution)/shard_map/all_gather | solution.py:288
  7.9 212.4 %all-gather.6.cloned.1.call-start = ((), (), s32[]{:S(2)}) async-start(), calls=%async_computation.4 | async-start | bytes 4456448 | tf_op jit(solution)/shard_map/all_gather | solution.py:289
  8.7 220.3 %all-gather.8.cloned.1.call-start = ((), (), s32[]{:S(2)}) async-start(), calls=%async_computation.6 | async-start | bytes 4456448 | tf_op jit(solution)/shard_map/all_gather | solution.py:290
  9.4 280.7 %reduce-scatter.8.cloned.1.call-start = ((), (), s32[]{:S(2)}) async-start(), calls=%async_computation.8 | async-start | bytes 3538944 | tf_op jit(solution)/shard_map/reduce_scatter | solution.py:310
  10.2 1.3 copy-start.2
  11.5 1.3 copy-start.3
  12.7 0.7 copy-start.6
  216.9 1.0 copy-start.4
  228.9 7.8 %copy-start.8 = (bf16[2048,1024]{1,0:T(8,128)(2,1)S(1)}, bf16[2048,1024]{1,0:T(8,128)(2,1)}, u32[]{:S(2)}) copy-start(bf16[2048,1024]{1,0:T(8,128)(2,1)} %all-gather.6.cloned.1.call-done) | copy-start | bytes 12582916
  236.7 3.5 copy-start.11
  236.7 3.5 copy-start.12
  236.7 3.7 copy-start.10
  236.8 3.9 copy-start.9
  245.4 139.3 %reduce-scatter.6.cloned.1.call-start = ((), (), s32[]{:S(2)}) async-start(), calls=%async_computation.7 | async-start | bytes 4456448 | tf_op jit(solution)/shard_map/reduce_scatter | solution.py:316
  253.0 207.9 %reduce-scatter.4.cloned.1.call-start = ((), (), s32[]{:S(2)}) async-start(), calls=%async_computation.5 | async-start | bytes 4456448 | tf_op jit(solution)/shard_map/reduce_scatter | solution.py:312
  259.1 31.0 %copy-start.7 = (s32[16]{0:T(128)S(1)}, s32[16]{0:T(128)}, u32[]{:S(2)}) copy-start(s32[16]{0:T(128)} %refs_0_.3) | copy-start | bytes 196
  259.1 86.4 %copy-start.5 = (bf16[3,512,384]{2,1,0:T(8,128)(2,1)S(1)}, bf16[3,512,384]{2,1,0:T(8,128)(2,1)}, u32[]{:S(2)}) copy-start(bf16[3,512,384]{2,1,0:T(8,128)(2,1)} %copy-done.4) | copy-start | bytes 3538948
  290.1 1.3 copy-start.1
Sparse Core Ops, SparseCore 0:
  9.6 38.7 all-gather.3
  50.5 90.1 all-gather.5
  142.9 71.2 all-gather.7
  245.6 44.5 reduce-scatter.7
  294.9 89.8 reduce-scatter.5
  389.1 71.8 reduce-scatter.3

commit v3 on v2

--- a/solution.py
+++ b/solution.py
@@ -288,7 +288,7 @@
     gathered = lax.all_gather(old[0], "dp", axis=1, tiled=True)
     x_rows = lax.all_gather(tokens, "expert", axis=0, tiled=True)
     cot_rows = lax.all_gather(cotangent, "expert", axis=0, tiled=True)
-    *old_here, gate_all = move_states(old, partner, gate_table, 0)
+    w_here, m_here, gate_all = move_states(old[:2], partner, gate_table, 0)
     gate = gate_all[:, 0, :].reshape(experts_here * tok_dev, 1)
     gate_up = jnp.concatenate([gathered[0], gathered[1]], axis=1)
     down_proj = gathered[2]
@@ -298,6 +298,12 @@
     sigmoid_pre = jax.nn.sigmoid(pre_act)
     silu_pre = pre_act * sigmoid_pre
     hidden = (silu_pre * lin_act).astype(bf16)
+    out_rows = jnp.dot(hidden, down_proj.T, preferred_element_type=f32)
+    out_part = (gate * out_rows).astype(bf16)
+    out_part, v_old = lax.optimization_barrier((out_part, old[2]))
+    mixed = lax.psum_scatter(out_part, "expert", scatter_dimension=0, tiled=True)
+    (v_here,) = move_states([v_old], partner, None, 2)
+    gate, v_here = lax.optimization_barrier((gate, v_here))
     dy_rows = (gate * cot_rows.astype(f32)).astype(bf16)
     hidden_grad = jnp.dot(dy_rows, down_proj, preferred_element_type=f32)
     pre_grad = hidden_grad * lin_act * sigmoid_pre * (1.0 + pre_act * (1.0 - sigmoid_pre))
@@ -307,15 +313,12 @@
     proj_grad = jnp.dot(x_rows.T, both_grad, preferred_element_type=f32).astype(bf16)
     down_grad = jnp.dot(dy_rows.T, hidden, preferred_element_type=f32).astype(bf16)
     partial = jnp.stack([proj_grad[:, :hidden_width], proj_grad[:, hidden_width:], down_grad])
+    partial, mixed = lax.optimization_barrier((partial, mixed))
     grad_sum = lax.psum_scatter(partial, "dp", scatter_dimension=1, tiled=True)
-    out_rows = jnp.dot(hidden, down_proj.T, preferred_element_type=f32)
-    mixed = lax.psum_scatter(
-        (gate * out_rows).astype(bf16), "expert", scatter_dimension=0, tiled=True
-    )
     item_grad = jnp.dot(both_grad, gate_up.T, preferred_element_type=f32).astype(bf16)
     token_grad = lax.psum_scatter(item_grad, "expert", scatter_dimension=0, tiled=True)
     (grad_here,) = move_states([grad_sum], partner, None, 1)
-    new_state = adam(*[a.astype(f32) for a in old_here], grad_here.astype(f32))
+    new_state = adam(*[a.astype(f32) for a in (w_here, m_here, v_here)], grad_here.astype(f32))
     outs = [a.astype(bf16).transpose(1, 0, 2)[None] for a in new_state]
     return (mixed, token_grad, *outs)
 

time: 468 us -> 421 us (0.90)
  waiting for transfers between devices: 144 us -> 100 us
  Pallas kernels: 258 us -> 253 us
    reduce_scatter x1, waiting for transfers between devices: 76.2 us -> 35.2 us  [shards_dense(): lax.psum_scatter(out_part, 'expert', scatter_dimension=0, tiled=True)]
    pallas_call x2 -> x3, Pallas kernels: 258 us -> 253 us  [move_states(): pl.pallas_call(functools.partial(move_kernel, n, count, bool(extra)), out...]
  transfers between devices with their start and end apart: 6 -> 6, of which waited for: 3 -> 3; matrix products, arithmetic and copies ran while one was open for 6% -> 10% of each run, Pallas kernels for 55% -> 60%
where the time goes in v3:
time: 421 us
  Pallas kernels  253 us (60%)
  waiting for transfers between devices  100 us (24%)
  matrix products  33.1 us (8%)
  between operations  14.4 us (3%)
  local copies, waits for them, and re-layouts  11 us (3%)
  other arithmetic  7.95 us (2%)
    pallas_call x3, Pallas kernels, move_states(): pl.pallas_call(functools.partial(move_kernel, n, count, bool(extra)), out...  253 us
    reduce_scatter x1, waiting for transfers between devices, shards_dense(): lax.psum_scatter(out_part, 'expert', scatter_dimension=0, tiled=True)  35.2 us
    reduce_scatter x1, waiting for transfers between devices, shards_dense(): lax.psum_scatter(item_grad, 'expert', scatter_dimension=0, tiled=True)  34.7 us
    reduce_scatter x1, waiting for transfers between devices, shards_dense(): grad_sum = lax.psum_scatter(partial, 'dp', scatter_dimension=1, tiled=True)  27.9 us
    unnamed x36, local copies, waits for them, and re-layouts  9.3 us
  transfers between devices with their start and end apart: 6, of which 3 were waited for; matrix products, arithmetic and copies ran while one was open for 10% of the time, Pallas kernels for 60%

profile of v3, /device:TPU:0, one launch (start us, length us, event | category | flops | bytes accessed | tf_op | source)
XLA Modules:
  0.0 420.5 jit_solution(2255723898985478249)
XLA Ops:
  9.4 0.7 select_reduce_fusion
  10.2 1.3 copy-done.3
  12.1 127.5 %shard_map.119 = (bf16[3,512,384]{2,1,0:T(8,128)(2,1)S(1)}, bf16[3,512,384]{2,1,0:T(8,128)(2,1)S(1)}, f32[16,8,128]{2,1,0:T(8,128)S(1)}) custom-call(s32[16]{0:T(128)S(1)} %copy-done.6, bf16[3,512,384]{2,1,0:T(8,128)(2,1)S(1)} %bitcast.51, bf16[3,512,384]{2,1,0:T(8,128)(2,1)S(1)} %bitcast.53, f32[16,8,128]{2,1,0:T(8,128)S(1)} %broadcast_in_dim.32.refs_3_), custom_call_target="tpu_custom_call" | custom-call | bytes 141557760 | tf_op jit(solution)/shard_map/pallas_call | solution.py:258
  139.7 1.0 copy-done.4
  140.7 1.5 slice_bitcast_fusion.4
  142.3 5.9 %convolution_bitcast_fusion = f32[2048,768]{0,1:T(8,128)S(1)} fusion(bf16[2048,1024]{1,0:T(8,128)(2,1)} %all-gather.6.cloned.1.call-done, bf16[1024,384]{1,0:T(8,128)(2,1)S(1)} %get-tuple-element.29, bf16[1024,384]{1,0:T(8,128)(2,1)S(1)} %get-tuple-element.28), kind=kOutput, calls=%fused_computation.2 | convolution fusion | flops 3224371200 | bytes 12058624 | tf_op jit(solution)/shard_map/dot_general | solution.py:295
  148.2 1.0 multiply_convert_fusion.4
  149.2 1.6 copy-done.8
  150.9 1.2 copy-done.9
  152.0 5.5 %multiply_convert_fusion.1 = bf16[2048,1024]{1,0:T(8,128)(2,1)} fusion(bf16[2048,384]{0,1:T(8,128)(2,1)S(1)} %multiply_convert_fusion.4, f32[2048]{0:T(1024)S(1)} %bitcast.57, bf16[3,1024,384]{2,1,0:T(8,128)(2,1)} %all-gather.4.cloned.1.call-done), kind=kOutput, calls=%fused_computation.1 | convolution fusion | flops 1614807040 | bytes 6561792 | tf_op jit(solution)/shard_map/dot_general | solution.py:301
  157.8 1.0 copy-done.1
  158.9 71.8 %shard_map.120 = bf16[3,512,384]{2,1,0:T(8,128)(2,1)S(1)} custom-call(s32[16]{0:T(128)S(1)} %copy-done.7, bf16[3,512,384]{2,1,0:T(8,128)(2,1)S(1)} %bitcast.52), custom_call_target="tpu_custom_call" | custom-call | bytes 70778880 | tf_op jit(solution)/shard_map/pallas_call | solution.py:258
  230.7 7.6 %multiply_convert_fusion.3 = (bf16[2048,384]{0,1:T(8,128)(2,1)S(1)}, bf16[2048,384]{0,1:T(8,128)(2,1)S(1)}) fusion(f32[2048,768]{0,1:T(8,128)} %copy-done.8, bf16[3,1024,384]{2,1,0:T(8,128)(2,1)} %all-gather.4.cloned.1.call-done, bf16[2048,1024]{1,0:T(8,128)(2,1)} %all-gather.8.cloned.1.call-done, f32[2048]{0:T(1024)S(1)} %bitcast.55), kind=kOutput, calls=%fused_computation.7 | convolution fusion | flops 1627127808 | bytes 14426112 | tf_op jit(solution)/shard_map/dot_general | solution.py:308
  238.4 3.5 fusion.12
  242.1 1.2 copy-done.10
  243.3 2.8 fusion.14
  246.1 1.8 pad_maximum_fusion.1
  247.9 35.2 %reduce-scatter.4.cloned.1.call-done = bf16[128,1024]{1,0:T(8,128)(2,1)} async-done(((bf16[2048,1024]{1,0:T(8,128)(2,1)}), bf16[128,1024]{1,0:T(8,128)(2,1)}) %reduce-scatter.4.cloned.1.call-update) | async-done | bytes 262160 | tf_op jit(solution)/shard_map/reduce_scatter | solution.py:304
  283.4 7.8 %convolution_convert_fusion = bf16[2048,1024]{1,0:T(8,128)(2,1)} fusion(bf16[2048,384]{0,1:T(8,128)(2,1)} %copy-done.17, bf16[2048,384]{0,1:T(8,128)(2,1)} %copy-done.16, bf16[1024,384]{1,0:T(8,128)(2,1)} %copy-done.13, bf16[1024,384]{1,0:T(8,128)(2,1)S(1)} %copy-done.12), kind=kOutput, calls=%fused_computation.3 | convolution fusion | flops 3232759808 | bytes 8912896 | tf_op jit(solution)/shard_map/dot_general | solution.py:318
  291.2 27.9 %reduce-scatter.8.cloned.1.call-done.refs_1_ = bf16[3,512,384]{2,1,0:T(8,128)(2,1)} async-done(((bf16[3,1024,384]{2,1,0:T(8,128)(2,1)}), bf16[3,512,384]{2,1,0:T(8,128)(2,1)}) %reduce-scatter.8.cloned.1.call-update) | async-done | bytes 1179664 | tf_op jit(solution)/shard_map/reduce_scatter | solution.py:317
  319.1 1.3 copy-done.2
  320.4 54.1 %shard_map.121 = bf16[3,512,384]{2,1,0:T(8,128)(2,1)S(1)} custom-call(s32[16]{0:T(128)S(1)} %copy-done.7, bf16[3,512,384]{2,1,0:T(8,128)(2,1)S(1)} %copy-done.2), custom_call_target="tpu_custom_call" | custom-call | bytes 70778880 | tf_op jit(solution)/shard_map/pallas_call | solution.py:258
  374.5 4.5 %fusion.15 = (bf16[1,512,3,384]{3,1,2,0:T(8,128)(2,1)}, bf16[1,512,3,384]{3,1,2,0:T(8,128)(2,1)}, bf16[1,512,3,384]{3,1,2,0:T(8,128)(2,1)}) fusion(bf16[3,512,384]{2,1,0:T(8,128)(2,1)S(1)} %shard_map.121, bf16[3,512,384]{2,1,0:T(8,128)(2,1)S(1)} %shard_map.120, bf16[3,512,384]{2,1,0:T(8,128)(2,1)S(1)} %copy-done.5, bf16[3,512,384]{2,1,0:T(8,128)(2,1)S(1)} %get-tuple-element.19), kind=kLoop, calls=%fused_computation.30 | loop fusion | flops 12976128 | bytes 8257536 | tf_op jit(solution)/shard_map/broadcast_in_dim | solution.py:322
  379.0 34.7 %reduce-scatter.6.cloned.1.call-done = bf16[128,1024]{1,0:T(8,128)(2,1)} async-done(((bf16[2048,1024]{1,0:T(8,128)(2,1)}), bf16[128,1024]{1,0:T(8,128)(2,1)}) %reduce-scatter.6.cloned.1.call-update) | async-done | bytes 262160 | tf_op jit(solution)/shard_map/reduce_scatter | solution.py:319
  (47 shorter events, 3.7 us)
Async XLA Ops:
  7.2 3.0 copy-start
  7.2 133.5 %all-gather.4.cloned.1.call-start = ((), (), s32[]{:S(2)}) async-start(), calls=%async_computation.3 | async-start | bytes 3538944 | tf_op jit(solution)/shard_map/all_gather | solution.py:288
  7.9 134.4 %all-gather.6.cloned.1.call-start = ((), (), s32[]{:S(2)}) async-start(), calls=%async_computation.4 | async-start | bytes 4456448 | tf_op jit(solution)/shard_map/all_gather | solution.py:289
  8.7 222.0 %all-gather.8.cloned.1.call-start = ((), (), s32[]{:S(2)}) async-start(), calls=%async_computation.5 | async-start | bytes 4456448 | tf_op jit(solution)/shard_map/all_gather | solution.py:290
  9.4 273.7 %reduce-scatter.4.cloned.1.call-start = ((), (), s32[]{:S(2)}) async-start(), calls=%async_computation.6 | async-start | bytes 4456448 | tf_op jit(solution)/shard_map/reduce_scatter | solution.py:304
  10.2 1.3 copy-start.3
  11.5 0.7 copy-start.6
  139.6 1.0 copy-start.4
  142.2 6.0 %copy-start.11 = (bf16[1024,384]{1,0:T(8,128)(2,1)}, bf16[1024,384]{1,0:T(8,128)(2,1)S(1)}, u32[]{:S(2)}) copy-start(bf16[1024,384]{1,0:T(8,128)(2,1)S(1)} %get-tuple-element.28) | copy-start | bytes 2359300
  142.2 6.0 %copy-start.13 = (bf16[1024,384]{1,0:T(8,128)(2,1)}, bf16[1024,384]{1,0:T(8,128)(2,1)S(1)}, u32[]{:S(2)}) copy-start(bf16[1024,384]{1,0:T(8,128)(2,1)S(1)} %get-tuple-element.29) | copy-start | bytes 2359300
  148.2 2.6 copy-start.8
  150.9 1.2 copy-start.9
  157.6 1.3 copy-start.1
  157.6 1.3 copy-start.7
  157.6 161.5 %reduce-scatter.8.cloned.1.call-start = ((), (), s32[]{:S(2)}) async-start(), calls=%async_computation.8 | async-start | bytes 3538944 | tf_op jit(solution)/shard_map/reduce_scatter | solution.py:317
  230.7 7.7 %copy-start.14 = (bf16[2048,1024]{1,0:T(8,128)(2,1)S(1)}, bf16[2048,1024]{1,0:T(8,128)(2,1)}, u32[]{:S(2)}) copy-start(bf16[2048,1024]{1,0:T(8,128)(2,1)} %all-gather.6.cloned.1.call-done) | copy-start | bytes 12582916
  238.3 3.5 copy-start.16
  238.4 3.5 copy-start.17
  238.4 3.7 copy-start.15
  241.9 1.4 copy-start.10
  247.9 35.5 %copy-start.12 = (bf16[1024,384]{1,0:T(8,128)(2,1)S(1)}, bf16[1024,384]{1,0:T(8,128)(2,1)}, u32[]{:S(2)}) copy-start(bf16[1024,384]{1,0:T(8,128)(2,1)} %copy-done.11) | copy-start | bytes 2359300
  283.1 130.6 %reduce-scatter.6.cloned.1.call-start = ((), (), s32[]{:S(2)}) async-start(), calls=%async_computation.7 | async-start | bytes 4456448 | tf_op jit(solution)/shard_map/reduce_scatter | solution.py:319
  291.2 83.3 %copy-start.5 = (bf16[3,512,384]{2,1,0:T(8,128)(2,1)S(1)}, bf16[3,512,384]{2,1,0:T(8,128)(2,1)}, u32[]{:S(2)}) copy-start(bf16[3,512,384]{2,1,0:T(8,128)(2,1)} %copy-done.4) | copy-start | bytes 3538948
  319.1 1.3 copy-start.2
Sparse Core Ops, SparseCore 0:
  9.6 38.7 all-gather.3
  50.5 82.1 all-gather.5
  134.9 67.8 all-gather.7
  207.0 76.0 reduce-scatter.3
  285.3 33.8 reduce-scatter.7
  323.4 90.2 reduce-scatter.5

commit v4 on v3

--- a/solution.py
+++ b/solution.py
@@ -285,7 +285,12 @@
     gate_table = jnp.sum(jnp.where(hits, gate_weights[:, :, None], 0.0), axis=1).T
     gate_table = jnp.broadcast_to(gate_table[:, None, :], (experts_here, 8, tok_dev))
     old = [a[0].transpose(1, 0, 2) for a in (weights, first_moment, second_moment)]
-    gathered = lax.all_gather(old[0], "dp", axis=1, tiled=True)
+    swap = [(0, 1), (1, 0)]
+    half = lax.axis_index("dp")
+    w_other = lax.ppermute(old[0], "dp", swap)
+    low = jnp.where(half == 0, old[0], w_other)
+    high = jnp.where(half == 0, w_other, old[0])
+    gathered = jnp.concatenate([low, high], axis=1)
     x_rows = lax.all_gather(tokens, "expert", axis=0, tiled=True)
     cot_rows = lax.all_gather(cotangent, "expert", axis=0, tiled=True)
     w_here, m_here, gate_all = move_states(old[:2], partner, gate_table, 0)
@@ -314,7 +319,9 @@
     down_grad = jnp.dot(dy_rows.T, hidden, preferred_element_type=f32).astype(bf16)
     partial = jnp.stack([proj_grad[:, :hidden_width], proj_grad[:, hidden_width:], down_grad])
     partial, mixed = lax.optimization_barrier((partial, mixed))
-    grad_sum = lax.psum_scatter(partial, "dp", scatter_dimension=1, tiled=True)
+    keep = lax.dynamic_slice_in_dim(partial, half * own_rows, own_rows, axis=1)
+    give = lax.dynamic_slice_in_dim(partial, (1 - half) * own_rows, own_rows, axis=1)
+    grad_sum = (keep.astype(f32) + lax.ppermute(give, "dp", swap).astype(f32)).astype(bf16)
     item_grad = jnp.dot(both_grad, gate_up.T, preferred_element_type=f32).astype(bf16)
     token_grad = lax.psum_scatter(item_grad, "expert", scatter_dimension=0, tiled=True)
     (grad_here,) = move_states([grad_sum], partner, None, 1)
@@ -325,7 +332,7 @@
 
 def shards(*args):
     replica_rows = lax.axis_size("expert") * args[0].shape[0]
-    if replica_rows <= 4096 and args[5].shape[1] % (16 * lax.axis_size("expert")) == 0:
+    if lax.axis_size("dp") == 2 and replica_rows <= 4096 and args[5].shape[1] % (16 * lax.axis_size("expert")) == 0:
         return shards_dense(*args)
     return shards_by_slot(*args)
 

time: 421 us -> 410 us (0.974)
  the two profiles are of different devices: /device:TPU:0 before, /device:TPU:29 now
where the time goes in v4:
time: 410 us
  Pallas kernels  307 us (75%)
  matrix products  32.7 us (8%)
  waiting for transfers between devices  29.2 us (7%)
  between operations  14 us (3%)
  other arithmetic  12.8 us (3%)
  local copies, waits for them, and re-layouts  12.2 us (3%)
    pallas_call x3, Pallas kernels, move_states(): pl.pallas_call(functools.partial(move_kernel, n, count, bool(extra)), out...  307 us
    ppermute x1, waiting for transfers between devices, shards_dense(): lax.ppermute(give, 'dp', swap).astype(f32)  27.8 us
    unnamed x36, local copies, waits for them, and re-layouts  9.9 us
  transfers between devices with their start and end apart: 6, of which 1 were waited for; matrix products, arithmetic and copies ran while one was open for 12% of the time, Pallas kernels for 75%

profile of v4, /device:TPU:29, one launch (start us, length us, event | category | flops | bytes accessed | tf_op | source)
XLA Modules:
  0.0 409.8 jit_solution(3729562354337166679)
XLA Ops:
  8.7 1.3 collective-permute-start
  10.7 1.3 copy-done
  12.0 1.3 copy-done.2
  13.9 160.3 %shard_map.119 = (bf16[3,512,384]{2,1,0:T(8,128)(2,1)S(1)}, bf16[3,512,384]{2,1,0:T(8,128)(2,1)S(1)}, f32[16,8,128]{2,1,0:T(8,128)S(1)}) custom-call(s32[16]{0:T(128)S(1)} %copy-done.5, bf16[3,512,384]{2,1,0:T(8,128)(2,1)S(1)} %bitcast.53, bf16[3,512,384]{2,1,0:T(8,128)(2,1)S(1)} %bitcast.55, f32[16,8,128]{2,1,0:T(8,128)S(1)} %broadcast_in_dim.32.refs_3_), custom_call_target="tpu_custom_call" | custom-call | bytes 141557760 | tf_op jit(solution)/shard_map/pallas_call | solution.py:258
  174.9 1.5 broadcast_select_fusion
  176.4 1.5 fusion.21
  177.9 5.7 %convolution_bitcast_fusion = f32[2048,768]{0,1:T(8,128)S(1)} fusion(bf16[2048,1024]{1,0:T(8,128)(2,1)} %all-gather.3.cloned.1.call-done, bf16[1024,384]{1,0:T(8,128)(2,1)} %get-tuple-element.29, bf16[1024,384]{1,0:T(8,128)(2,1)} %get-tuple-element.28), kind=kOutput, calls=%fused_computation.2 | convolution fusion | flops 3224371200 | bytes 12058624 | tf_op jit(solution)/shard_map/dot_general | solution.py:300
  184.6 1.6 copy-done.7
  186.2 1.1 copy-done.10
  187.4 4.4 %multiply_convert_fusion.1 = bf16[2048,1024]{1,0:T(8,128)(2,1)} fusion(bf16[2048,384]{0,1:T(8,128)(2,1)S(1)} %multiply_convert_fusion.4, f32[2048]{0:T(1024)S(1)} %bitcast.59, bf16[3,512,384]{2,1,0:T(8,128)(2,1)S(1)} %get-tuple-element.30, bf16[3,512,384]{2,1,0:T(8,128)(2,1)S(1)} %get-tuple-element.31), kind=kOutput, calls=%fused_computation.1 | convolution fusion | flops 1616379904 | bytes 8134656 | tf_op jit(solution)/shard_map/dot_general | solution.py:306
  192.1 1.0 copy-done.1
  193.1 72.9 %shard_map.120 = bf16[3,512,384]{2,1,0:T(8,128)(2,1)S(1)} custom-call(s32[16]{0:T(128)S(1)} %copy-done.6, bf16[3,512,384]{2,1,0:T(8,128)(2,1)S(1)} %bitcast.54), custom_call_target="tpu_custom_call" | custom-call | bytes 70778880 | tf_op jit(solution)/shard_map/pallas_call | solution.py:258
  266.1 7.7 %multiply_convert_fusion.3 = (bf16[2048,384]{0,1:T(8,128)(2,1)S(1)}, bf16[2048,384]{0,1:T(8,128)(2,1)S(1)}) fusion(f32[2048,768]{0,1:T(8,128)} %copy-done.7, bf16[3,512,384]{2,1,0:T(8,128)(2,1)} %copy-done.8, bf16[3,512,384]{2,1,0:T(8,128)(2,1)} %copy-done.9, bf16[2048,1024]{1,0:T(8,128)(2,1)} %all-gather.5.cloned.1.call-done, f32[2048]{0:T(1024)S(1)} %bitcast.57), kind=kOutput, calls=%fused_computation.7 | convolution fusion | flops 1628700672 | bytes 15998976 | tf_op jit(solution)/shard_map/dot_general | solution.py:313
  273.8 1.2 copy-done.16
  275.5 5.1 %convolution_convert_fusion = bf16[2048,1024]{1,0:T(8,128)(2,1)} fusion(bf16[2048,384]{0,1:T(8,128)(2,1)S(1)} %get-tuple-element.24, bf16[2048,384]{0,1:T(8,128)(2,1)S(1)} %get-tuple-element.23, bf16[1024,384]{1,0:T(8,128)(2,1)S(1)} %copy-done.13, bf16[1024,384]{1,0:T(8,128)(2,1)S(1)} %copy-done.12), kind=kOutput, calls=%fused_computation.3 | convolution fusion | flops 3232759808 | bytes 8912896 | tf_op jit(solution)/shard_map/dot_general | solution.py:325
  280.7 6.8 %fusion.12 = bf16[1024,768]{1,0:T(8,128)(2,1)S(1)} fusion(bf16[2048,1024]{1,0:T(8,128)(2,1)} %all-gather.3.cloned.1.call-done, bf16[2048,384]{0,1:T(8,128)(2,1)} %copy-done.17, bf16[2048,384]{0,1:T(8,128)(2,1)} %copy-done.16), kind=kOutput, calls=%fused_computation.32 | convolution fusion | flops 3228303360 | bytes 8912896 | tf_op jit(solution)/shard_map/dot_general | solution.py:318
  287.6 1.2 copy-done.11
  288.8 2.8 fusion.14
  291.7 1.7 pad_maximum_fusion.1
  293.4 1.5 constant_dynamic-slice_fusion
  295.3 27.8 %collective-permute-done.1 = bf16[3,512,384]{2,1,0:T(8,128)(2,1)} collective-permute-done((bf16[3,512,384]{2,1,0:T(8,128)(2,1)S(1)}, bf16[3,512,384]{2,1,0:T(8,128)(2,1)}, u32[]{:S(2)}, u32[]{:S(2)}) %collective-permute-start.1) | collective-permute-done | bytes 1179680 | tf_op jit(solution)/shard_map/ppermute | solution.py:324
  323.0 1.9 add_convert_fusion.refs_1_
  324.9 73.8 %shard_map.121 = bf16[3,512,384]{2,1,0:T(8,128)(2,1)S(1)} custom-call(s32[16]{0:T(128)S(1)} %copy-done.6, bf16[3,512,384]{2,1,0:T(8,128)(2,1)S(1)} %add_convert_fusion.refs_1_), custom_call_target="tpu_custom_call" | custom-call | bytes 70778880 | tf_op jit(solution)/shard_map/pallas_call | solution.py:258
  398.7 4.5 %fusion.15 = (bf16[1,512,3,384]{3,1,2,0:T(8,128)(2,1)}, bf16[1,512,3,384]{3,1,2,0:T(8,128)(2,1)}, bf16[1,512,3,384]{3,1,2,0:T(8,128)(2,1)}) fusion(bf16[3,512,384]{2,1,0:T(8,128)(2,1)S(1)} %shard_map.121, bf16[3,512,384]{2,1,0:T(8,128)(2,1)S(1)} %shard_map.120, bf16[3,512,384]{2,1,0:T(8,128)(2,1)S(1)} %copy-done.4, bf16[3,512,384]{2,1,0:T(8,128)(2,1)S(1)} %get-tuple-element.19), kind=kLoop, calls=%fused_computation.35 | loop fusion | flops 12976128 | bytes 8257536 | tf_op jit(solution)/shard_map/broadcast_in_dim | solution.py:329
  (48 shorter events, 5.9 us)
Async XLA Ops:
  7.2 170.7 %all-gather.3.cloned.1.call-start = ((), (), s32[]{:S(2)}) async-start(), calls=%async_computation.2 | async-start | bytes 4456448 | tf_op jit(solution)/shard_map/all_gather | solution.py:294
  7.9 258.1 %all-gather.5.cloned.1.call-start = ((), (), s32[]{:S(2)}) async-start(), calls=%async_computation.3 | async-start | bytes 4456448 | tf_op jit(solution)/shard_map/all_gather | solution.py:295
  8.6 284.8 %reduce-scatter.3.cloned.1.call-start = ((), (), s32[]{:S(2)}) async-start(), calls=%async_computation.4 | async-start | bytes 4456448 | tf_op jit(solution)/shard_map/reduce_scatter | solution.py:309
  8.7 166.2 %collective-permute-start = (bf16[3,512,384]{2,1,0:T(8,128)(2,1)}, bf16[3,512,384]{2,1,0:T(8,128)(2,1)}, u32[]{:S(2)}, u32[]{:S(2)}) collective-permute-start(bf16[3,512,384]{2,1,0:T(8,128)(2,1)} %bitcast.52), channel_id=1, source_target_pairs={{0,16},{16,0},{1,17},{17,1},{2,18},{18,2},{3,19},{19,3},{4,20},{20... | collective-permute-start | bytes 3538952 | tf_op jit(solution)/shard_map/ppermute | solution.py:290
  10.7 1.3 copy-start
  12.0 1.3 copy-start.2
  13.3 0.7 copy-start.5
  174.2 2.2 copy-start.3
  176.4 9.9 %copy-start.8 = (bf16[3,512,384]{2,1,0:T(8,128)(2,1)}, bf16[3,512,384]{2,1,0:T(8,128)(2,1)S(1)}, u32[]{:S(2)}) copy-start(bf16[3,512,384]{2,1,0:T(8,128)(2,1)S(1)} %get-tuple-element.30) | copy-start | bytes 3538948
  176.4 9.9 %copy-start.9 = (bf16[3,512,384]{2,1,0:T(8,128)(2,1)}, bf16[3,512,384]{2,1,0:T(8,128)(2,1)S(1)}, u32[]{:S(2)}) copy-start(bf16[3,512,384]{2,1,0:T(8,128)(2,1)S(1)} %get-tuple-element.31) | copy-start | bytes 3538948
  183.6 2.6 copy-start.7
  183.6 3.8 copy-start.14
  186.2 1.2 copy-start.10
  191.8 1.3 copy-start.1
  191.8 1.3 copy-start.6
  191.8 211.4 %reduce-scatter.5.cloned.1.call-start = ((), (), s32[]{:S(2)}) async-start(), calls=%async_computation.5 | async-start | bytes 4456448 | tf_op jit(solution)/shard_map/reduce_scatter | solution.py:326
  266.0 9.4 %copy-start.12 = (bf16[1024,384]{1,0:T(8,128)(2,1)S(1)}, bf16[1024,384]{1,0:T(8,128)(2,1)}, u32[]{:S(2)}) copy-start(bf16[1024,384]{1,0:T(8,128)(2,1)} %get-tuple-element.28) | copy-start | bytes 2359300
  266.0 9.4 %copy-start.13 = (bf16[1024,384]{1,0:T(8,128)(2,1)S(1)}, bf16[1024,384]{1,0:T(8,128)(2,1)}, u32[]{:S(2)}) copy-start(bf16[1024,384]{1,0:T(8,128)(2,1)} %get-tuple-element.29) | copy-start | bytes 2359300
  273.8 1.2 copy-start.16
  273.8 1.7 copy-start.17
  280.6 7.0 %copy-start.15 = (bf16[2048,1024]{1,0:T(8,128)(2,1)S(1)}, bf16[2048,1024]{1,0:T(8,128)(2,1)}, u32[]{:S(2)}) copy-start(bf16[2048,1024]{1,0:T(8,128)(2,1)} %all-gather.5.cloned.1.call-done) | copy-start | bytes 12582916
  287.4 1.4 copy-start.11
  294.9 28.1 %collective-permute-start.1 = (bf16[3,512,384]{2,1,0:T(8,128)(2,1)S(1)}, bf16[3,512,384]{2,1,0:T(8,128)(2,1)}, u32[]{:S(2)}, u32[]{:S(2)}) collective-permute-start(bf16[3,512,384]{2,1,0:T(8,128)(2,1)S(1)} %constant_dynamic-slice_fusion), channel_id=1, source_target_pairs={{0,16},{16,0},{1,17},{17,1},{2,18},{18,2},{3,19},{19,3},{4,20},{20... | collective-permute-start | bytes 3538952 | tf_op jit(solution)/shard_map/ppermute | solution.py:324
  295.3 103.5 %copy-start.4 = (bf16[3,512,384]{2,1,0:T(8,128)(2,1)S(1)}, bf16[3,512,384]{2,1,0:T(8,128)(2,1)}, u32[]{:S(2)}) copy-start(bf16[3,512,384]{2,1,0:T(8,128)(2,1)} %copy-done.3) | copy-start | bytes 3538948
Sparse Core Ops, SparseCore 0:
  10.2 97.1 all-gather.2
  109.5 64.7 all-gather.4
  192.0 86.5 reduce-scatter.2
  283.3 105.4 reduce-scatter.4
